TPU v7x, 32 devices: a whole 2x2x4 slice. The times are simulated.
32 devices in a mesh: wide: 8 (over z, y), narrow: 4 (over x, core).
Axes of the slice: x: 2, y: 2, z: 4, core: 2. Of those that a mesh axis runs over, the one named last changes fastest.
Arguments:
- tokens: bfloat16 [4096, 2048], P('wide'), may hold values from -6 to 6
- cotangent: bfloat16 [4096, 2048], P('wide'), may hold values from -6 to 6
- keep_mask: int32 [4096], P('wide'), may hold values 0 or 1
- doc_lengths: int32 [1, 16], replicated, may hold values from 1 to 2048, 4096 in all within a row
- block_order: int32 [1, 16], replicated, may hold values from 0 to 15, each once within a row
- gain_attn: bfloat16 [2048], replicated, may hold values from 0.25 to 1.75
- w_query: bfloat16 [2048, 2048], P(None, 'narrow'), may hold values from -0.125 to 0.125
- w_key: bfloat16 [2048, 1024], P(None, 'narrow'), may hold values from -0.125 to 0.125
- w_value: bfloat16 [2048, 1024], P(None, 'narrow'), may hold values from -0.125 to 0.125
- w_out: bfloat16 [2048, 2048], P('narrow'), may hold values from -0.5 to 0.5
- gain_dense: bfloat16 [2048], replicated, may hold values from 0.25 to 1.75
- w_gate: bfloat16 [2048, 5632], P(None, 'narrow'), may hold values from -0.125 to 0.125
- w_up: bfloat16 [2048, 5632], P(None, 'narrow'), may hold values from -0.125 to 0.125
- w_down: bfloat16 [5632, 2048], P('narrow'), may hold values from -0.078125 to 0.078125
Outputs:
- output: bfloat16 [4096, 2048], P('wide')
- grad_tokens: bfloat16 [4096, 2048], P('wide')
- grad_gain_attn: float32 [2048], P('wide')
- grad_w_query: float32 [2048, 2048], P('wide', 'narrow')
- grad_w_key: float32 [2048, 1024], P('wide', 'narrow')
- grad_w_value: float32 [2048, 1024], P('wide', 'narrow')
- grad_w_out: float32 [2048, 2048], P('narrow', 'wide')
- grad_gain_dense: float32 [2048], P('wide')
- grad_w_gate: float32 [2048, 5632], P('wide', 'narrow')
- grad_w_up: float32 [2048, 5632], P('wide', 'narrow')
- grad_w_down: float32 [5632, 2048], P('narrow', 'wide')
All inputs are finite; a program needn't handle non-finite values. No bound on the sum of `keep_mask` on one device may be relied on, other than what follows from the above.
Results may differ from a plain program's by a relative error of at most 0.025.
Values may be sent and summed in bfloat16 or wider, within the bound.
No kernel may reach another device: no remote copies, remote signals or barrier semaphores. Data moves between devices by JAX's collectives and lax.ppermute only.
A program may use at most 192 MiB of HBM per device.

v0:
```python
import functools

import jax
import jax.numpy as jnp
import numpy as np
from jax import lax
from jax.experimental import pallas as pl
from jax.experimental.pallas import tpu as pltpu
from jax.sharding import PartitionSpec as P

HD = 128
EPSILON = 1e-05
NEGATIVE = -1e30
BASE = 10000.0
LOG2E = 1.4426950408889634
SCORE = HD ** (-0.5) * LOG2E
FACTOR = HD ** (-0.5)
BF = jnp.bfloat16
F32 = jnp.float32
NT = (((1,), (1,)), ((), ()))
TN = (((0,), (0,)), ((), ()))
NN = (((1,), (0,)), ((), ()))
VM = pl.BlockSpec(memory_space=pltpu.VMEM)
SM = pl.BlockSpec(memory_space=pltpu.SMEM)
ANY = pl.BlockSpec(memory_space=pl.ANY)


def dot(a, b, dims=(((1,), (0,)), ((), ()))):
    return lax.dot_general(a, b, dims, preferred_element_type=F32)


def narrow_swap(value, mask):
    pairs = [(n, n ^ mask) for n in range(lax.axis_size("narrow"))]
    return lax.ppermute(value, "narrow", pairs)


def wide_swap(value):
    return lax.ppermute(value, "wide", [(w, w ^ 1) for w in range(lax.axis_size("wide"))])


def wide_ring(value, group, hop=1):
    ring = group // 2
    pairs = []
    for w in range(lax.axis_size("wide")):
        base, member = w // group * group, w % group
        pairs.append((w, base + (member // 2 + hop) % ring * 2 + member % 2))
    return lax.ppermute(value, "wide", pairs)


def wide_flip(value, bit):
    return lax.ppermute(value, "wide", [(w, w ^ (2 << bit)) for w in range(lax.axis_size("wide"))])


def halving(count):
    groups = []
    step = 1
    while step < count:
        groups.append([k for k in range(count) if k % (2 * step) == step])
        step *= 2
    return [*groups, [0]]


def stretches(groups):
    starts, at = [], 0
    for group in groups:
        starts.append((at, len(group)))
        at += len(group)
    return starts


def rope(value, cosine, sine):
    return value * cosine + pltpu.roll(value, HD // 2, 1) * sine


def norm_kv_kernel(core, x_ref, gain_ref, wk_ref, wv_ref, cos_ref, sin_ref, normed_ref, *kv_refs):
    x = x_ref[...].astype(F32)
    scale = lax.rsqrt(jnp.mean(x * x, axis=1, keepdims=True) + EPSILON)
    normed = (x * scale * gain_ref[...].astype(F32)).astype(BF)
    normed_ref[...] = normed
    keys = dot(normed, wk_ref[...])
    values = dot(normed, wv_ref[...])
    for h, ref in enumerate(kv_refs):
        cols = slice(h * HD, (h + 1) * HD)
        ref[:, :HD] = rope(keys[:, cols], cos_ref[...], sin_ref[...]).astype(BF)
        ref[:, HD:] = values[:, cols].astype(BF)


def norm_kv(core, tokens, gain, wk, wv, cosine, sine):
    rows, width = tokens.shape
    half = rows // 2
    heads = wk.shape[1] // HD
    full = lambda w: pl.BlockSpec(w.shape, lambda i, c: (0, 0))
    outs = pl.pallas_call(
        norm_kv_kernel,
        out_shape=[jax.ShapeDtypeStruct((rows, width), BF)]
        + [jax.ShapeDtypeStruct((rows, 2 * HD), BF)] * heads,
        grid_spec=pltpu.PrefetchScalarGridSpec(
            num_scalar_prefetch=1,
            grid=(2,),
            in_specs=[
                pl.BlockSpec((half, width), lambda i, c: (i ^ c[0], 0)),
                full(gain),
                full(wk),
                full(wv),
                pl.BlockSpec((half, HD), lambda i, c: (i, 0)),
                pl.BlockSpec((half, HD), lambda i, c: (i, 0)),
            ],
            out_specs=[pl.BlockSpec((half, width), lambda i, c: (i, 0))]
            + [pl.BlockSpec((half, 2 * HD), lambda i, c: (i, 0))] * heads,
        ),
        cost_estimate=pl.CostEstimate(flops=int(2.9e9), bytes_accessed=0, transcendentals=0),
        name="norm_kv",
    )(core, tokens, gain, wk, wv, cosine, sine)
    return outs[0], outs[1:]


def query_kernel(x_ref, w_ref, cos_ref, sin_ref, out_ref):
    raw = dot(x_ref[...], w_ref[...])
    for h in range(raw.shape[1] // HD):
        cols = slice(h * HD, (h + 1) * HD)
        out_ref[:, cols] = rope(raw[:, cols], cos_ref[...], sin_ref[...]).astype(BF)


def query_proj(x, w, cosine, sine):
    rows, width = x.shape
    half = rows // 2
    return pl.pallas_call(
        query_kernel,
        out_shape=jax.ShapeDtypeStruct((rows, w.shape[1]), BF),
        grid=(2,),
        in_specs=[
            pl.BlockSpec((half, width), lambda i: (i, 0)),
            pl.BlockSpec(w.shape, lambda i: (0, 0)),
            pl.BlockSpec((half, HD), lambda i: (i, 0)),
            pl.BlockSpec((half, HD), lambda i: (i, 0)),
        ],
        out_specs=pl.BlockSpec((half, w.shape[1]), lambda i: (i, 0)),
        cost_estimate=pl.CostEstimate(flops=int(2.9e9), bytes_accessed=0, transcendentals=0),
        name="query_proj",
    )(x, w, cosine, sine)


def fetch_slots(slot_refs, slots, kv_ref, sems):
    rows, width = slot_refs[0].shape
    copies = []
    for at, ref in enumerate(slot_refs):
        head, slot = divmod(at, slots)
        spot = kv_ref.at[pl.ds(slot * rows, rows), pl.ds(head * width, width)]
        copies.append(pltpu.make_async_copy(ref, spot, sems.at[at]))
    for copy in copies:
        copy.start()
    for copy in copies:
        copy.wait()


def allowed(pk, size, span, pos, low):
    key_pos = pk * size + lax.broadcasted_iota(jnp.int32, (size, span), 0)
    return (key_pos <= pos) & (key_pos >= low)


def attn_fwd_kernel(slots, *refs):
    meta, q_ref, pos_ref, low_ref = refs[:4]
    slot_refs = refs[4 : 4 + slots]
    mixed_ref, lse_ref, kv_ref, acc_ref, sems = refs[-5:]
    fetch_slots(slot_refs, slots, kv_ref, sems)
    size = q_ref.shape[0] // 2
    for i in range(2):
        rows = slice(i * size, (i + 1) * size)
        pos = jnp.tile(pos_ref[0:1, rows], (1, 2))
        low = jnp.tile(low_ref[0:1, rows], (1, 2))
        queries = [q_ref[rows, r * HD : (r + 1) * HD] for r in range(2)]
        acc_ref[...] = jnp.zeros_like(acc_ref)

        def body(pk, carry):
            peak, total = carry
            spot = pl.multiple_of(meta[4 + pk] * size, size)
            keys = kv_ref[pl.ds(spot, size), :HD]
            values = kv_ref[pl.ds(spot, size), HD:]
            scores = jnp.concatenate([dot(keys, q, NT) for q in queries], axis=1) * SCORE
            scores = jnp.where(allowed(pk, size, 2 * size, pos, low), scores, NEGATIVE)
            peak_new = jnp.maximum(peak, jnp.max(scores, axis=0, keepdims=True))
            alpha = jnp.exp2(peak - peak_new)
            probs = jnp.exp2(scores - peak_new)
            total = total * alpha + jnp.sum(probs, axis=0, keepdims=True)
            acc_ref[...] = acc_ref[...] * alpha + dot(values, probs.astype(BF), TN)
            return peak_new, total

        start = (jnp.full((1, 2 * size), NEGATIVE, F32), jnp.zeros((1, 2 * size), F32))
        peak, total = lax.fori_loop(meta[i], meta[2 + i] + 1, body, start)
        lse_ref[i : i + 1, :] = peak + jnp.log2(total)
        out = acc_ref[...] * (1.0 / total)
        for r in range(2):
            mixed_ref[rows, r * HD : (r + 1) * HD] = out[:, r * size : (r + 1) * size].T.astype(BF)


def attn_fwd(head, meta, q, pos, low, slots, mixed):
    rows = q.shape[0]
    count = len(slots)
    earlier = [] if mixed is None else [mixed]
    return pl.pallas_call(
        functools.partial(attn_fwd_kernel, count),
        out_shape=(
            jax.ShapeDtypeStruct(q.shape, BF),
            jax.ShapeDtypeStruct((2, rows), F32),
        ),
        grid=(1,),
        in_specs=[
            SM,
            pl.BlockSpec((rows, 2 * HD), lambda i: (0, head)),
            pl.BlockSpec(pos.shape, lambda i: (0, 0)),
            pl.BlockSpec(low.shape, lambda i: (0, 0)),
        ]
        + [ANY] * (count + len(earlier)),
        out_specs=[
            pl.BlockSpec((rows, 2 * HD), lambda i: (0, head)),
            pl.BlockSpec((2, rows), lambda i: (0, 0)),
        ],
        input_output_aliases={4 + count: 0} if earlier else {},
        scratch_shapes=[
            pltpu.VMEM((count * rows, 2 * HD), BF),
            pltpu.VMEM((HD, rows), F32),
            pltpu.SemaphoreType.DMA((count,)),
        ],
        cost_estimate=pl.CostEstimate(flops=int(1e9), bytes_accessed=0, transcendentals=0),
        name="attn_fwd",
    )(meta, q, pos, low, *slots, *earlier)


def attn_bwd_kernel(heads, slots, groups, *refs):
    meta, q_ref, pos_ref, low_ref, dmix_ref, mixed_ref, cos_ref, sin_ref = refs[:8]
    lse_refs = refs[8 : 8 + heads]
    at = 8 + heads
    slot_refs = refs[at : at + heads * slots]
    at += heads * slots
    dq_ref, dkv_refs = refs[at], refs[at + 1 : -4]
    kv_ref, dkv_ref, dq_acc, sems = refs[-4:]
    fetch_slots(slot_refs, slots, kv_ref, sems)
    dkv_ref[...] = jnp.zeros_like(dkv_ref)
    rows_all = q_ref.shape[0]
    size = rows_all // 2
    for i in range(2):
        rows = slice(i * size, (i + 1) * size)
        pos = jnp.tile(pos_ref[0:1, rows], (1, 2))
        low = jnp.tile(low_ref[0:1, rows], (1, 2))
        for g in range(heads):
            cols = [slice((2 * g + r) * HD, (2 * g + r + 1) * HD) for r in range(2)]
            queries = jnp.concatenate([q_ref[rows, c] for c in cols], axis=0)
            grads = jnp.concatenate([dmix_ref[rows, c] for c in cols], axis=0)
            outs = jnp.concatenate([mixed_ref[rows, c] for c in cols], axis=0)
            delta = jnp.sum((grads.astype(F32) * outs.astype(F32)).T, axis=0, keepdims=True)
            lse = lse_refs[g][i : i + 1, :]
            dq_acc[...] = jnp.zeros_like(dq_acc)

            def body(pk, carry):
                spot = pl.multiple_of(meta[4 + pk] * size, size)
                key_cols = slice(2 * g * HD, (2 * g + 1) * HD)
                value_cols = slice((2 * g + 1) * HD, (2 * g + 2) * HD)
                keys = kv_ref[pl.ds(spot, size), key_cols]
                values = kv_ref[pl.ds(spot, size), value_cols]
                scores = dot(keys, queries, NT) * SCORE
                probs = jnp.where(
                    allowed(pk, size, 2 * size, pos, low), jnp.exp2(scores - lse), 0.0
                )
                d_probs = dot(values, grads, NT)
                d_scores = (probs * (d_probs - delta)).astype(BF)
                dkv_ref[pl.ds(spot, size), value_cols] += dot(probs.astype(BF), grads)
                dkv_ref[pl.ds(spot, size), key_cols] += dot(d_scores, queries) * FACTOR
                dq_acc[...] += dot(d_scores, keys, TN)
                return carry

            lax.fori_loop(meta[i], meta[2 + i] + 1, body, 0)
            for r in range(2):
                part = dq_acc[r * size : (r + 1) * size, :] * FACTOR
                dq_ref[rows, cols[r]] = rope(part, cos_ref[rows, :], -sin_ref[rows, :]).astype(BF)
    ring = slots // 2
    for j, ref in enumerate(dkv_refs):
        first = ring * (j // len(groups))
        for place, k in enumerate(groups[j % len(groups)]):
            spot = pl.multiple_of((first + meta[4 + 2 * slots + k]) * rows_all, rows_all)
            ref[place * rows_all : (place + 1) * rows_all, :] = dkv_ref[
                pl.ds(spot, rows_all), :
            ].astype(BF)


def attn_bwd(meta, q, pos, low, lse, mixed, dmix, cosine, sine, slots):
    rows, q_width = q.shape
    heads, count = len(slots), len(slots[0])
    kv_width = heads * 2 * HD
    groups = halving(count // 2)
    outs = pl.pallas_call(
        functools.partial(attn_bwd_kernel, heads, count, groups),
        out_shape=[jax.ShapeDtypeStruct((rows, q_width), BF)]
        + [jax.ShapeDtypeStruct((len(g) * rows, kv_width), BF) for g in groups] * 2,
        in_specs=[SM] + [VM] * (7 + heads) + [ANY] * (heads * count),
        out_specs=[VM] * (1 + 2 * len(groups)),
        scratch_shapes=[
            pltpu.VMEM((count * rows, kv_width), BF),
            pltpu.VMEM((count * rows, kv_width), F32),
            pltpu.VMEM((rows, HD), F32),
            pltpu.SemaphoreType.DMA((heads * count,)),
        ],
        cost_estimate=pl.CostEstimate(flops=int(2e9), bytes_accessed=0, transcendentals=0),
        name="attn_bwd",
    )(meta, q, pos, low, dmix, mixed, cosine, sine, *lse, *[v for head in slots for v in head])
    return outs[0], outs[1 : 1 + len(groups)], outs[1 + len(groups) :]


def cost(micros):
    return pl.CostEstimate(flops=int(micros * 0.3e9), bytes_accessed=0, transcendentals=0)


def split_rows(total, own_ref, other_ref):
    half = own_ref.shape[0]
    own_ref[...] = total[:half].astype(BF)
    other_ref[...] = total[half:].astype(BF)


def project_kernel(spec, *refs):
    total = None
    for a, b, offset, dims in spec:
        left = refs[a][...] if dims is not None else None
        if dims == "nt":
            right, form = refs[b][:, offset : offset + left.shape[1]], NT
        else:
            right, form = refs[b][offset : offset + left.shape[1], :], NN
        term = dot(left, right, form)
        total = term if total is None else total + term
    split_rows(total, refs[-2], refs[-1])


def project(pairs, dims, tile, micros):
    operands, specs, plan, weights = [], [], [], []
    for a, b, offset in pairs:
        operands.append(a)
        specs.append(pl.BlockSpec(a.shape, lambda i: (0, 0)))
        spot = next((at for at, seen in weights if seen is b), None)
        left = len(operands) - 1
        if spot is None:
            spot = len(operands)
            operands.append(b)
            weights.append((spot, b))
            if dims == "nt":
                specs.append(pl.BlockSpec((tile, b.shape[1]), lambda i: (i, 0)))
            else:
                specs.append(pl.BlockSpec((b.shape[0], tile), lambda i: (0, i)))
        plan.append((left, spot, offset, dims))
    rows = pairs[0][0].shape[0]
    width = pairs[0][1].shape[0 if dims == "nt" else 1]
    return pl.pallas_call(
        functools.partial(project_kernel, plan),
        out_shape=[jax.ShapeDtypeStruct((rows // 2, width), BF)] * 2,
        grid=(width // tile,),
        in_specs=specs,
        out_specs=[pl.BlockSpec((rows // 2, tile), lambda i: (0, i))] * 2,
        cost_estimate=cost(micros),
        name="project",
    )(*operands)


def back_dense_kernel(gate_a, up_a, gate_b, up_b, wg_ref, wu_ref, own_ref, other_ref):
    total = None
    offset = 0
    for group in ((gate_a, up_a), (gate_b, up_b)):
        count = group[0].shape[1]
        for ref, w_ref in zip(group, (wg_ref, wu_ref)):
            term = dot(ref[...], w_ref[:, offset : offset + count], NT)
            total = term if total is None else total + term
        offset += count
    split_rows(total, own_ref, other_ref)


def back_dense(grads, w_gate, w_up, tile, part, parts):
    width, hidden = w_gate.shape[0] // parts, w_gate.shape[1]
    rows = grads[0].shape[0]
    ahead = part * (width // tile)
    weight = pl.BlockSpec((tile, hidden), lambda i: (ahead + i, 0))
    return pl.pallas_call(
        back_dense_kernel,
        out_shape=[jax.ShapeDtypeStruct((rows // 2, width), BF)] * 2,
        grid=(width // tile,),
        in_specs=[pl.BlockSpec(v.shape, lambda i: (0, 0)) for v in grads] + [weight, weight],
        out_specs=[pl.BlockSpec((rows // 2, tile), lambda i: (0, i))] * 2,
        cost_estimate=cost(11 / parts),
        name="back_dense",
    )(*grads, w_gate, w_up)


def gated_kernel(own_ref, other_ref, wg_ref, wu_ref, di_ref, inner_ref, dg_ref, du_ref, all_ref):
    @pl.when(pl.program_id(0) == 0)
    def _():
        half = own_ref.shape[0]
        all_ref[:half, :] = own_ref[...]
        all_ref[half:, :] = other_ref[...]

    gate = dot(all_ref[...], wg_ref[...])
    up = dot(all_ref[...], wu_ref[...])
    sigma = 1.0 / (1.0 + jnp.exp(-gate))
    silu = gate * sigma
    d_inner = di_ref[...]
    inner_ref[...] = (silu * up).astype(BF)
    dg_ref[...] = (d_inner * up * sigma * (1.0 + gate * (1.0 - sigma))).astype(BF)
    du_ref[...] = (d_inner * silu).astype(BF)


def gated(own, other, wg, wu, d_inner, first, columns, tile):
    half, width = own.shape
    weight = pl.BlockSpec((width, tile), lambda i: (0, first // tile + i))
    whole = pl.BlockSpec((half, width), lambda i: (0, 0))
    return pl.pallas_call(
        gated_kernel,
        out_shape=[jax.ShapeDtypeStruct((2 * half, columns), BF)] * 3,
        grid=(pl.cdiv(columns, tile),),
        in_specs=[
            whole,
            whole,
            weight,
            weight,
            pl.BlockSpec((2 * half, tile), lambda i: (0, first // tile + i)),
        ],
        out_specs=[pl.BlockSpec((2 * half, tile), lambda i: (0, i))] * 3,
        scratch_shapes=[pltpu.VMEM((2 * half, width), BF)],
        cost_estimate=cost(7.5),
        name="gated",
    )(own, other, wg, wu, d_inner)


def mixed_grad_kernel(own_ref, other_ref, w_ref, out_ref):
    both = jnp.concatenate([own_ref[...], other_ref[...]], axis=0)
    out_ref[...] = dot(both, w_ref[...], NT).astype(BF)


def mixed_grad(own, other, w):
    return pl.pallas_call(
        mixed_grad_kernel,
        out_shape=jax.ShapeDtypeStruct((2 * own.shape[0], w.shape[0]), BF),
        in_specs=[VM] * 3,
        out_specs=VM,
        cost_estimate=cost(4),
        name="mixed_grad",
    )(own, other, w)


def d_inner_kernel(x_ref, w_ref, out_ref):
    out_ref[...] = dot(x_ref[...], w_ref[...], NT)


def inner_grad(x, w, tile):
    rows, width = x.shape
    hidden = w.shape[0]
    return pl.pallas_call(
        d_inner_kernel,
        out_shape=jax.ShapeDtypeStruct((rows, hidden), F32),
        grid=(pl.cdiv(hidden, tile),),
        in_specs=[
            pl.BlockSpec((rows, width), lambda i: (0, 0)),
            pl.BlockSpec((tile, width), lambda i: (i, 0)),
        ],
        out_specs=pl.BlockSpec((rows, tile), lambda i: (0, i)),
        cost_estimate=cost(8),
        name="inner_grad",
    )(x, w)


def pack_kernel(count, plan, strip, tbl, *refs):
    ins, outs = refs[:count], refs[count:]
    for out_ref, pieces in zip(outs, plan):
        column = 0
        for at, rows, row in pieces:
            for k in range(tbl.shape[1]):
                first = pl.multiple_of(tbl[row, k] * strip, 128)
                out_ref[:, column : column + strip] = ins[at][rows, pl.ds(first, strip)]
                column += strip


def pack(values, plan, tbl, strip):
    turns = tbl.shape[1]
    if strip % 128:
        cut = lambda v, rows, at: lax.dynamic_slice_in_dim(v[rows], at * strip, strip, axis=1)
        return [
            jnp.concatenate(
                [cut(values[at], rows, tbl[row, k]) for at, rows, row in pieces for k in range(turns)],
                axis=1,
            )
            for pieces in plan
        ]
    return pl.pallas_call(
        functools.partial(pack_kernel, len(values), plan, strip),
        out_shape=[
            jax.ShapeDtypeStruct(
                (p[0][1].stop - p[0][1].start, len(p) * turns * strip), values[0].dtype
            )
            for p in plan
        ],
        in_specs=[SM] + [VM] * len(values),
        out_specs=[VM] * len(plan),
        cost_estimate=cost(1.5),
        name="pack",
    )(tbl, *values)


def strip_rows_kernel(halves, near, rights, nears, spans, tbl, *refs):
    left = refs[:halves]
    left_near = refs[halves : halves + near]
    right = refs[halves + near : halves + near + rights]
    right_near = refs[halves + near + rights : halves + near + rights + nears]
    outs = refs[halves + near + rights + nears :]
    step = pl.program_id(0)
    join = lambda group: (
        group[0][...] if len(group) == 1 else jnp.concatenate([r[...] for r in group], axis=0)
    )
    mine, theirs = join(left), join(left_near)
    pieces = []
    for r, n in zip(right, right_near):
        planes = range(r.shape[0]) if len(r.shape) == 3 else [None]
        for k in planes:
            a = r[...] if k is None else r[k]
            b = n[...] if k is None else n[k]
            pieces.append((dot(mine, a, TN) + dot(theirs, b, TN)).astype(BF))
    for (start, length), out in zip(spans, outs):

        @pl.when((step >= start) & (step < start + length))
        def _(out=out):
            column = 0
            for piece in pieces:
                out[:, column : column + piece.shape[1]] = piece
                column += piece.shape[1]


def strip_rows_grad(left, left_near, right, right_near, tbl, strip, micros):
    turns = tbl.shape[1]
    columns = sum(r.shape[-1] * (r.shape[0] if r.ndim == 3 else 1) for r in right)
    spans = stretches(halving(turns))
    if strip % 128:
        near = jnp.concatenate(left_near, axis=0)
        mine = jnp.concatenate(left, axis=0)
        flat = lambda r: [r] if r.ndim == 2 else [r[k] for k in range(r.shape[0])]
        outs = []
        for start, length in spans:
            group = []
            for k in range(start, start + length):
                a = lax.dynamic_slice_in_dim(mine, tbl[0, k] * strip, strip, axis=1)
                b = near[:, k * strip : (k + 1) * strip]
                group.append(
                    jnp.concatenate(
                        [
                            dot(a, x, TN) + dot(b, y, TN)
                            for r, n in zip(right, right_near)
                            for x, y in zip(flat(r), flat(n))
                        ],
                        axis=1,
                    ).astype(BF)
                )
            outs.append(jnp.concatenate(group, axis=0))
        return outs
    held = lambda start, length: (lambda i, t: (jnp.clip(i - start, 0, length - 1), 0))
    whole = lambda v: pl.BlockSpec(v.shape, lambda i, t: (0,) * v.ndim)
    return pl.pallas_call(
        functools.partial(
            strip_rows_kernel, len(left), len(left_near), len(right), len(right_near), spans
        ),
        out_shape=[jax.ShapeDtypeStruct((length * strip, columns), BF) for _, length in spans],
        grid_spec=pltpu.PrefetchScalarGridSpec(
            num_scalar_prefetch=1,
            grid=(turns,),
            in_specs=[pl.BlockSpec((v.shape[0], strip), lambda i, t: (0, t[0, i])) for v in left]
            + [pl.BlockSpec((v.shape[0], strip), lambda i, t: (0, i)) for v in left_near]
            + [whole(v) for v in [*right, *right_near]],
            out_specs=[pl.BlockSpec((strip, columns), held(*span)) for span in spans],
        ),
        cost_estimate=cost(micros),
        name="strip_rows",
    )(tbl, *left, *left_near, *right, *right_near)


def strip_columns_kernel(parts, halves, near, strip, spans, *refs):
    at = 2 * parts
    right, right_near = refs[at : at + halves], refs[at + halves : at + halves + near]
    outs = refs[at + halves + near :]
    first = 0
    for p in range(parts):
        total = None
        for ref, group in ((refs[p], right), (refs[parts + p], right_near)):
            row = 0
            for r in group:
                term = dot(ref[row : row + r.shape[0], :], r[...], TN)
                total = term if total is None else total + term
                row += r.shape[0]
        for (start, length), out in zip(spans, outs):
            out[first : first + total.shape[0], :] = total[
                :, start * strip : (start + length) * strip
            ].astype(BF)
        first += total.shape[0]


def strip_columns_grad(left, left_near, right, right_near, turns, strip, tile, micros, near_at=0):
    rows, count = left[0].shape[0], sum(v.shape[1] for v in left)
    if strip * turns % 128:
        raise ValueError(strip)
    spans = stretches(halving(turns))
    whole = lambda v: pl.BlockSpec(v.shape, lambda i: (0, 0))
    near = lambda v: pl.BlockSpec((v.shape[0], turns * strip), lambda i: (0, near_at))
    if len(left) == 1:
        left_specs = [pl.BlockSpec((rows, tile), lambda i: (0, i))] * 2
    else:
        tile = count
        left_specs = [whole(v) for v in [*left, *left_near]]
    return pl.pallas_call(
        functools.partial(
            strip_columns_kernel, len(left), len(right), len(right_near), strip, spans
        ),
        out_shape=[jax.ShapeDtypeStruct((count, length * strip), BF) for _, length in spans],
        grid=(pl.cdiv(count, tile),),
        in_specs=left_specs + [whole(v) for v in right] + [near(v) for v in right_near],
        out_specs=[pl.BlockSpec((tile, length * strip), lambda i: (i, 0)) for _, length in spans],
        cost_estimate=cost(micros),
        name="strip_columns",
    )(*left, *left_near, *right, *right_near)


def close_kv_kernel(count, *refs):
    cos_ref, sin_ref, dk_ref, dv_ref = refs[count:]
    total = refs[0][...].astype(F32)
    for ref in refs[1:count]:
        total = total + ref[...].astype(F32)
    heads = dk_ref.shape[1] // HD
    for h in range(heads):
        cols = slice(h * HD, (h + 1) * HD)
        keys = total[:, 2 * h * HD : (2 * h + 1) * HD]
        dk_ref[:, cols] = rope(keys, cos_ref[...], -sin_ref[...]).astype(BF)
        dv_ref[:, cols] = total[:, (2 * h + 1) * HD : (2 * h + 2) * HD].astype(BF)


def close_kv(terms, cosine, sine):
    rows, width = terms[0].shape
    first = lambda w: pl.BlockSpec((rows, w), lambda i: (0, 0))
    return pl.pallas_call(
        functools.partial(close_kv_kernel, len(terms)),
        out_shape=[jax.ShapeDtypeStruct((rows, width // 2), BF)] * 2,
        grid=(1,),
        in_specs=[first(width)] * len(terms) + [first(HD)] * 2,
        out_specs=[first(width // 2)] * 2,
        cost_estimate=cost(1.5),
        name="close_kv",
    )(*terms, cosine, sine)


def norm_backward(source, scale_rows, gain, upstream):
    weighted = upstream * gain
    average = jnp.mean(weighted * source, axis=1, keepdims=True)
    return scale_rows * weighted - source * scale_rows**3 * average


def after(value, *done):
    return lax.optimization_barrier((value, *done))[0]


def shards(
    tokens,
    cotangent,
    keep_mask,
    doc_lengths,
    block_order,
    gain_attn,
    w_query,
    w_key,
    w_value,
    w_out,
    gain_dense,
    w_gate,
    w_up,
    w_down,
):
    rows, width = tokens.shape
    half = rows // 2
    wide = lax.axis_size("wide")
    group = wide // block_order.shape[0]
    ring = group // 2
    wide_index = lax.axis_index("wide")
    member = wide_index % group
    seq_index = wide_index // group
    side = (wide_index % 2).astype(jnp.int32)
    core = lax.axis_index("narrow") % 2
    strip = width // wide
    turns = wide // 2

    def ordered(mine, other):
        return jnp.where(
            core == 0,
            jnp.concatenate([mine, other], axis=0),
            jnp.concatenate([other, mine], axis=0),
        )

    def own_half(value):
        return lax.dynamic_slice_in_dim(value, core * half, half)

    def other_half(value):
        return lax.dynamic_slice_in_dim(value, (1 - core) * half, half)

    order_row = lax.dynamic_index_in_dim(block_order, seq_index, 0, keepdims=False)
    length_row = lax.dynamic_index_in_dim(doc_lengths, seq_index, 0, keepdims=False)
    doc_ends = jnp.cumsum(length_row)
    places = jnp.stack([member * 2 + core, member * 2 + 1 - core])
    chosen = jnp.sum(
        jnp.where(places[:, None] == jnp.arange(2 * group)[None, :], order_row[None, :], 0), axis=1
    )
    pos = (chosen[:, None] * half + jnp.arange(half, dtype=jnp.int32)[None, :]).reshape(-1)
    low = jnp.max(jnp.where(doc_ends[None, :] <= pos[:, None], doc_ends[None, :], 0), axis=1)
    block_low = low.reshape(2, half)[:, 0] // half
    stored = jnp.sum(
        jnp.where(
            order_row[None, :] == jnp.arange(2 * group)[:, None], jnp.arange(2 * group)[None, :], 0
        ),
        axis=1,
    )
    owner = stored // 2
    slot = (member // 2 - owner // 2) % ring + ring * (owner % 2 != side).astype(jnp.int32)
    spots = slot * 2 + (stored % 2 != core).astype(jnp.int32)
    place = member // 2
    back = (place - (place ^ jnp.arange(ring, dtype=jnp.int32))) % ring
    meta = jnp.concatenate([block_low, chosen, spots, back]).astype(jnp.int32)
    frequency = BASE ** (-(jnp.arange(HD // 2, dtype=F32) * 2.0) / HD)
    angles = pos.astype(F32)[:, None] * frequency[None, :]
    cosine = jnp.cos(angles)
    sine = jnp.sin(angles)
    cosine = jnp.concatenate([cosine, cosine], axis=1)
    sine = jnp.concatenate([-sine, sine], axis=1)
    pos_row = pos[None, :]
    low_row = low[None, :]

    order = np.array([k for stretch in halving(turns) for k in stretch], np.int32)
    turn_row = wide_index // 2 ^ order
    tbl = jnp.stack([2 * turn_row + side, 2 * turn_row + 1 - side]).astype(jnp.int32)
    core_arr = core.astype(jnp.int32)[None]
    normed_one, both = norm_kv(core_arr, tokens, gain_attn[None, :], w_key, w_value, cosine, sine)
    low_rows, all_rows = slice(0, half), slice(0, rows)

    def together(*values):
        return list(lax.optimization_barrier(values))

    near, far = [[v] for v in both], [[] for v in both]
    query = d_dense = d_inner = input_near = d_dense_strips = None
    for step in range(ring):
        for head in range(len(both)):
            held = near[head][step]
            if step + 1 < ring:
                sent = [wide_swap(held), wide_ring(held, group)]
            elif head == 0:
                sent = [wide_swap(held)]
            else:
                sent = [wide_ring(far[head][0], group, -1)]
            beside = []
            if step == 0 and head == 0:
                beside = [query_proj(normed_one, w_query, cosine, sine)]
            if step == 0 and head == 1:
                keep_rel = jnp.concatenate([own_half(keep_mask), other_half(keep_mask)])[:, None]
                cot_rel = jnp.concatenate([own_half(cotangent), other_half(cotangent)])
                beside = [jnp.where(keep_rel > 0, cot_rel, jnp.zeros_like(cot_rel))]
            if step == 1 and head == 0:
                beside = [inner_grad(d_dense, w_down, 256)]
            if step == 2 and head == 0:
                beside = pack(
                    [normed_one, d_dense],
                    [[(0, low_rows, 1), (1, low_rows, 1)], [(1, all_rows, 0)]],
                    tbl,
                    strip,
                )
            done = together(*sent, *beside)
            far[head].append(done[0])
            if step + 1 < ring:
                near[head].append(done[1])
            if step == 0 and head == 0:
                query = done[-1]
            if step == 0 and head == 1:
                d_dense = done[-1]
            if step == 1 and head == 0:
                d_inner = done[-1]
            if step == 2 and head == 0:
                input_near, d_dense_strips = done[-2:]
    slots = [n + f for n, f in zip(near, far)]
    input_near = wide_swap(after(input_near, far[0][-2]))
    mixed, lse = None, []
    for h, held in enumerate(slots):
        mixed, part = attn_fwd(h, meta, query, pos_row, low_row, held, mixed)
        lse.append(part)

    def reduce_narrow(halves, hold=()):
        own_part, other_part = halves
        got = narrow_swap(other_part, 1)
        held = (own_part.astype(F32) + got.astype(F32)).astype(BF)
        return held, narrow_swap(held, 2)

    def total_of(held, got):
        return held.astype(F32) + got.astype(F32)

    part = project([(mixed, w_out, 0)], "nn", 1024, 4)
    held, got = reduce_narrow((part[0], after(part[1], input_near)))
    mixed_near = wide_swap(mixed)
    input_near_other = narrow_swap(input_near, 1)
    source = own_half(tokens).astype(F32)
    keep_own = own_half(keep_mask).astype(F32)[:, None]
    hidden_one = source + keep_own * total_of(held, got)
    gain_two = gain_dense.astype(F32)
    scale_two = lax.rsqrt(jnp.mean(hidden_one * hidden_one, axis=1, keepdims=True) + EPSILON)
    normed_two = (hidden_one * scale_two * gain_two).astype(BF)
    normed_two_other = narrow_swap(after(normed_two, mixed_near), 1)
    (normed_two_near,) = pack([normed_two], [[(0, low_rows, 1)]], tbl, strip)
    normed_two_near = wide_swap(normed_two_near)

    hidden = w_gate.shape[1]
    tile = 256
    first_count = 3 * tile
    inner_a, *dgu_a = gated(
        normed_two, normed_two_other, w_gate, w_up, d_inner, 0, first_count, tile
    )
    inner_a_near = wide_swap(inner_a)
    inner_b, *dgu_b = gated(
        after(normed_two, inner_a),
        normed_two_other,
        w_gate,
        w_up,
        d_inner,
        first_count,
        hidden - first_count,
        tile,
    )
    back = back_dense([*dgu_a, dgu_b[0], after(dgu_b[1], normed_two_near)], w_gate, w_up, 512, 0, 1)
    held, got = reduce_narrow((back[0], after(back[1], inner_a_near)))

    def halve(parts, axis, hold=None):
        groups = halving(1 << (len(parts) - 1))
        size = parts[-1].shape[axis]
        received, sent = [], None
        for bit, group in enumerate(groups[:-1]):
            sent = parts[bit]
            if bit:
                total = sent.astype(F32)
                for early, value in enumerate(received):
                    there = [k ^ (1 << early) for k in groups[early]]
                    pick = [
                        lax.slice_in_dim(value, size * there.index(k), size * (there.index(k) + 1), axis=axis)
                        for k in group
                    ]
                    total = total + (pick[0] if len(pick) == 1 else jnp.concatenate(pick, axis)).astype(F32)
                sent = total.astype(BF)
                if hold is not None:
                    sent = after(sent, hold)
            received.append(wide_flip(sent, bit))
        return received, sent

    def close(parts, received, axis):
        size = parts[-1].shape[axis]
        total = parts[-1].astype(F32)
        for value in received:
            total = total + lax.slice_in_dim(value, 0, size, axis=axis).astype(F32)
        return total

    near_sides = [input_near, input_near_other]
    down_a = strip_columns_grad(
        [after(inner_a, held)],
        [inner_a_near],
        [d_dense_strips],
        near_sides,
        turns,
        strip,
        tile,
        4,
        1,
    )
    inner_b_near = wide_swap(inner_b)
    normed_two_near_other = narrow_swap(after(normed_two_near, held), 1)
    down_a_got, down_a_mid = halve(down_a, 1)
    dgu_a_near = [wide_swap(after(v, inner_b)) for v in dgu_a]
    dense_parts = project(
        [(after(inner_a, down_a[0]), w_down, 0), (inner_b, w_down, first_count)], "nn", 512, 6
    )
    down_b = strip_columns_grad(
        [after(inner_b, dense_parts[0])], [inner_b_near], [d_dense_strips], near_sides, turns, strip, tile, 4, 1
    )

    got = after(got, dense_parts[0], down_b[0])
    down_b_got, down_b_mid = halve(down_b, 1, got)
    upstream = own_half(cotangent).astype(F32)
    d_hidden = upstream + norm_backward(hidden_one, scale_two, gain_two, total_of(held, got))
    d_attn = (keep_own * d_hidden).astype(BF)
    d_attn_other = narrow_swap(after(d_attn, dgu_a_near[0], down_a_mid), 1)

    d_mixed = mixed_grad(d_attn, d_attn_other, w_out)
    d_query, d_near, d_far = attn_bwd(
        meta, query, pos_row, low_row, lse, mixed, after(d_mixed, down_b_mid), cosine, sine, slots
    )
    held_out, got_out = reduce_narrow((dense_parts[0], after(dense_parts[1], d_mixed)))
    output_own = (hidden_one + keep_own * total_of(held_out, got_out)).astype(BF)
    output = ordered(output_own, narrow_swap(output_own, 1))

    d_far = [wide_swap(v) for v in d_far]
    normed_two_sides = [normed_two_near, normed_two_near_other]
    gate_up_a = strip_rows_grad(
        [after(normed_two, d_query, down_a_got[-1], down_b_got[-1]), normed_two_other], normed_two_sides, dgu_a, dgu_a_near, tbl, strip, 8
    )
    gate_up_a_got, gate_up_a_mid = halve(gate_up_a, 0, d_far[1])
    d_far[0] = after(d_far[0], gate_up_a_mid)
    pairs = [
        (n.astype(F32) + f.astype(F32)).astype(BF) for n, f in zip(d_near[:-1], d_far[:-1])
    ]
    kv_got, kv_mid = halve([*pairs, d_near[-1]], 0)
    d_key, d_value = close_kv([d_near[-1], d_far[-1], *kv_got], cosine, sine)

    dgu_b_near = [wide_swap(after(v, d_query)) for v in dgu_b]
    gate_up_b = strip_rows_grad(
        [after(normed_two, gate_up_a_mid, kv_mid), normed_two_other],
        normed_two_sides,
        dgu_b,
        dgu_b_near,
        tbl,
        strip,
        7,
    )
    d_query_near = wide_swap(after(d_query, pairs[0]))
    gate_up_b_got, gate_up_b_mid = halve(gate_up_b, 0)
    d_attn_near, d_attn_strips, d_attn_other_strips = pack(
        [after(d_attn, gate_up_a[0]), d_attn_other],
        [[(0, low_rows, 1)], [(0, low_rows, 0)], [(1, low_rows, 0)]],
        tbl,
        strip,
    )
    d_attn_near = wide_swap(after(d_attn_near, pairs[0]))
    d_attn_near_other = narrow_swap(d_attn_near, 1)
    query_part = strip_rows_grad(
        [after(normed_one, gate_up_b[0])], near_sides, [d_query], [d_query_near], tbl, strip, 4
    )
    query_got, query_mid = halve(query_part, 0)
    out_part = strip_columns_grad(
        [after(mixed, query_part[0])],
        [mixed_near],
        [d_attn_strips, d_attn_other_strips],
        [d_attn_near, d_attn_near_other],
        turns,
        strip,
        tile,
        4,
    )
    out_got, out_mid = halve(out_part, 1)

    kv_width = w_key.shape[1]
    held, got = reduce_narrow(
        project([(d_query, w_query, 0), (d_key, w_key, 0), (d_value, w_value, 0)], "nt", 512, 6)
    )
    gain_one = gain_attn.astype(F32)
    scale_one = lax.rsqrt(jnp.mean(source * source, axis=1, keepdims=True) + EPSILON)
    d_normed_one = total_of(held, got)
    grad_own = (d_hidden + norm_backward(source, scale_one, gain_one, d_normed_one)).astype(BF)
    grad_tokens = ordered(grad_own, narrow_swap(grad_own, 1))

    d_key_near = wide_swap(d_key)
    d_value_near = wide_swap(d_value)
    kv_part = strip_rows_grad(
        [after(normed_one, out_part[0])],
        near_sides,
        [d_key, d_value],
        [d_key_near, d_value_near],
        tbl,
        strip,
        4,
    )
    kv_part_got, _ = halve(kv_part, 0)
    grad_kv = close(kv_part, kv_part_got, 0)
    grad_down_a = close(down_a, down_a_got, 1)
    grad_down_b = close(down_b, down_b_got, 1)
    grad_gate_up_a = close(gate_up_a, gate_up_a_got, 0)
    grad_gate_up_b = close(gate_up_b, gate_up_b_got, 0)
    grad_query = close(query_part, query_got, 0)
    grad_out = close(out_part, out_got, 1)
    grad_key, grad_value = grad_kv[:, :kv_width], grad_kv[:, kv_width:]
    grad_down = jnp.concatenate([grad_down_a, grad_down_b], axis=0)
    second_count = hidden - first_count
    grad_gate = jnp.concatenate(
        [grad_gate_up_a[:, :first_count], grad_gate_up_b[:, :second_count]], axis=1
    )
    grad_up = jnp.concatenate(
        [grad_gate_up_a[:, first_count:], grad_gate_up_b[:, second_count:]], axis=1
    )

    def strip_rows(weight):
        return lax.dynamic_slice_in_dim(weight, wide_index * strip, strip).astype(F32)

    def gain_grad(pairs, gain):
        local = sum(jnp.sum(strip_rows(w) * g, axis=1) for w, g in pairs)
        return local / lax.dynamic_slice_in_dim(gain, wide_index * strip, strip)

    local = jnp.stack(
        [
            gain_grad([(w_query, grad_query), (w_key, grad_key), (w_value, grad_value)], gain_one),
            gain_grad([(w_gate, grad_gate), (w_up, grad_up)], gain_two),
        ]
    )
    local = local + narrow_swap(local, 1)
    local = local + narrow_swap(local, 2)
    grad_gain_one, grad_gain_two = local[0], local[1]
    return (
        output,
        grad_tokens,
        grad_gain_one,
        grad_query,
        grad_key,
        grad_value,
        grad_out,
        grad_gain_two,
        grad_gate,
        grad_up,
        grad_down,
    )


def solution(mesh):
    placed = (
        P("wide", None),
        P("wide", None),
        P("wide"),
        P(),
        P(),
        P(),
        P(None, "narrow"),
        P(None, "narrow"),
        P(None, "narrow"),
        P("narrow", None),
        P(),
        P(None, "narrow"),
        P(None, "narrow"),
        P("narrow", None),
    )
    return jax.shard_map(
        shards,
        mesh=mesh,
        in_specs=placed,
        out_specs=(
            P("wide", None),
            P("wide", None),
            P("wide"),
            P("wide", "narrow"),
            P("wide", "narrow"),
            P("wide", "narrow"),
            P("narrow", "wide"),
            P("wide"),
            P("wide", "narrow"),
            P("wide", "narrow"),
            P("narrow", "wide"),
        ),
        check_vma=False,
    )
```

profile of v0, /device:TPU:0, one launch (start us, length us, event | category | flops | bytes accessed | tf_op | source)
XLA Modules:
  0.0 543.4 jit_solution(6981832102902981359)
XLA Ops:
  28.6 8.5 %inner_grad.1.di_ref = f32[512,1408]{1,0:T(8,128)} custom-call(bf16[512,2048]{1,0:T(8,128)(2,1)} %maximum_select_fusion.x_ref.refs_1_, bf16[1408,2048]{1,0:T(8,128)(2,1)} %refs_1_.4), custom_call_target="tpu_custom_call" | custom-call | flops 2400000000 | tf_op jit(solution)/shard_map/inner_grad/pallas_call | solution.py:450
  60.0 20.7 %collective-permute-done.6.refs_10_.refs_24_ = bf16[512,256]{1,0:T(8,128)(2,1)S(1)} collective-permute-done((bf16[512,256]{1,0:T(8,128)(2,1)S(1)}, bf16[512,256]{1,0:T(8,128)(2,1)S(1)}, u32[]{:S(2)}, u32[]{:S(2)}) %collective-permute-start.6) | collective-permute-done | bytes 262176 | tf_op jit(solution)/shard_map/ppermute | solution.py:38
  84.2 6.9 %attn_fwd.2 = (bf16[512,512]{1,0:T(8,128)(2,1)}, f32[2,512]{1,0:T(2,128)}) custom-call(s32[24]{0:T(128)} %pad_add_fusion.2.refs_0_, bf16[512,512]{1,0:T(8,128)(2,1)} %query_proj.1.refs_1_, s32[1,512]{1,0:T(1,128)} %bitcast.32, s32[1,512]{1,0:T(1,128)} %bitcast.29, bf16[512,256]{1,0:T(8,128)(2,1)} %get-tuple-element.113.refs_4_.refs_10_, ...), custom_call_target="tpu_custom_call" | custom-call | flops 1000000000 | tf_op jit(solution)/shard_map/attn_fwd/pallas_call | solution.py:200
  91.2 7.5 %attn_fwd.3 = (bf16[512,512]{1,0:T(8,128)(2,1)}, f32[2,512]{1,0:T(2,128)}) custom-call(s32[24]{0:T(128)} %pad_add_fusion.2.refs_0_, bf16[512,512]{1,0:T(8,128)(2,1)} %query_proj.1.refs_1_, s32[1,512]{1,0:T(1,128)} %bitcast.33, s32[1,512]{1,0:T(1,128)} %bitcast.30, ...), custom_call_target="tpu_custom_call", output_to_operand_aliasing={{0}: (12, {})} | custom-call | flops 1000000000 | tf_op jit(solution)/shard_map/attn_fwd/pallas_call | solution.py:200
  108.6 23.6 %collective-permute-done.16 = bf16[256,2048]{1,0:T(8,128)(2,1)S(1)} collective-permute-done((bf16[256,2048]{1,0:T(8,128)(2,1)S(1)}, bf16[256,2048]{1,0:T(8,128)(2,1)S(1)}, u32[]{:S(2)}, u32[]{:S(2)}) %collective-permute-start.16) | collective-permute-done | bytes 1048608 | tf_op jit(solution)/shard_map/ppermute | solution.py:34
  137.7 8.2 %gated.2 = (bf16[512,768]{1,0:T(8,128)(2,1)}, bf16[512,768]{1,0:T(8,128)(2,1)}, bf16[512,768]{1,0:T(8,128)(2,1)}) custom-call(bf16[256,2048]{1,0:T(8,128)(2,1)} %multiply_convert_fusion.1.own_ref.refs_0_, bf16[256,2048]{1,0:T(8,128)(2,1)} %collective-permute-done.18.other_ref.refs_1_, bf16[2048,1408]{1,0:T(8,128)(2,1)} %wg_ref.5, bf16[2048,1408]{1,0:T(8,128)(2,1)} %wu_ref.5, ...), custom_call_target="tpu_custom_call" | custom-call | flops 2249999872 | tf_op jit(solution)/shard_map/gated/pallas_call | solution.py:409
  147.1 7.7 %gated.3 = (bf16[512,640]{1,0:T(8,128)(2,1)}, bf16[512,640]{1,0:T(8,128)(2,1)}, bf16[512,640]{1,0:T(8,128)(2,1)}) custom-call(bf16[256,2048]{1,0:T(8,128)(2,1)} %multiply_convert_fusion.1.own_ref.refs_0_, bf16[256,2048]{1,0:T(8,128)(2,1)} %collective-permute-done.18.other_ref.refs_1_, bf16[2048,1408]{1,0:T(8,128)(2,1)} %wg_ref.5, bf16[2048,1408]{1,0:T(8,128)(2,1)} %wu_ref.5, ...), custom_call_target="tpu_custom_call" | custom-call | flops 2249999872 | tf_op jit(solution)/shard_map/gated/pallas_call | solution.py:409
  154.8 10.8 %back_dense.1 = (bf16[256,2048]{1,0:T(8,128)(2,1)}, bf16[256,2048]{1,0:T(8,128)(2,1)}) custom-call(bf16[512,768]{1,0:T(8,128)(2,1)} %get-tuple-element.161.gate_a.refs_4_, bf16[512,768]{1,0:T(8,128)(2,1)} %get-tuple-element.177.up_a.refs_5_, bf16[512,640]{1,0:T(8,128)(2,1)} %get-tuple-element.189.gate_b.refs_4_, ...), custom_call_target="tpu_custom_call" | custom-call | flops 3300000000 | tf_op jit(solution)/shard_map/back_dense/pallas_call | solution.py:377
  184.0 7.1 %project.4 = (bf16[256,2048]{1,0:T(8,128)(2,1)}, bf16[256,2048]{1,0:T(8,128)(2,1)}) custom-call(bf16[512,768]{1,0:T(8,128)(2,1)} %get-tuple-element.154.refs_0_, bf16[1408,2048]{1,0:T(8,128)(2,1)} %refs_1_.4, bf16[512,640]{1,0:T(8,128)(2,1)} %get-tuple-element.158.refs_2_.refs_0_), custom_call_target="tpu_custom_call" | custom-call | flops 1800000000 | tf_op jit(solution)/shard_map/project/pallas_call | solution.py:349
  191.0 8.7 %collective-permute-done.24.refs_1_ = bf16[512,640]{1,0:T(8,128)(2,1)S(1)} collective-permute-done((bf16[512,640]{1,0:T(8,128)(2,1)}, bf16[512,640]{1,0:T(8,128)(2,1)S(1)}, u32[]{:S(2)}, u32[]{:S(2)}) %collective-permute-start.24) | collective-permute-done | bytes 655392 | tf_op jit(solution)/shard_map/ppermute | solution.py:38
  221.5 19.4 %collective-permute-done.31 = bf16[640,512]{1,0:T(8,128)(2,1)S(1)} collective-permute-done((bf16[640,512]{1,0:T(8,128)(2,1)S(1)}, bf16[640,512]{1,0:T(8,128)(2,1)S(1)}, u32[]{:S(2)}, u32[]{:S(2)}) %collective-permute-start.31) | collective-permute-done | bytes 655392 | tf_op jit(solution)/shard_map/ppermute | solution.py:51
  249.4 16.2 %attn_bwd.1 = (bf16[512,512]{1,0:T(8,128)(2,1)}, bf16[1024,512]{1,0:T(8,128)(2,1)}, bf16[512,512]{1,0:T(8,128)(2,1)}, bf16[512,512]{1,0:T(8,128)(2,1)}, bf16[102...) custom-call(s32[24]{0:T(128)} %pad_add_fusion.2.refs_0_, ...), custom_call_target="tpu_custom_call" | custom-call | flops 2000000000 | tf_op jit(solution)/shard_map/attn_bwd/pallas_call | solution.py:290
  265.7 9.3 %strip_rows.4 = (bf16[512,1536]{1,0:T(8,128)(2,1)}, bf16[256,1536]{1,0:T(8,128)(2,1)}, bf16[256,1536]{1,0:T(8,128)(2,1)}) custom-call(s32[2,4]{1,0:T(2,128)} %pad_add_fusion.tbl, bf16[256,2048]{1,0:T(8,128)(2,1)} %multiply_convert_fusion.1.own_ref.refs_0_, bf16[256,2048]{1,0:T(8,128)(2,1)} %collective-permute-done.18.other_ref.refs_1_, ...), custom_call_target="tpu_custom_call" | custom-call | flops 2400000000 | tf_op jit(solution)/shard_map/strip_rows/pallas_call | solution.py:557
  284.6 30.6 %collective-permute-done.38 = bf16[512,1536]{1,0:T(8,128)(2,1)S(1)} collective-permute-done((bf16[512,1536]{1,0:T(8,128)(2,1)}, bf16[512,1536]{1,0:T(8,128)(2,1)S(1)}, u32[]{:S(2)}, u32[]{:S(2)}) %collective-permute-start.38) | collective-permute-done | bytes 1572896 | tf_op jit(solution)/shard_map/ppermute | solution.py:51
  332.7 23.6 %collective-permute-done.40.refs_2_ = bf16[1024,512]{1,0:T(8,128)(2,1)} collective-permute-done((bf16[1024,512]{1,0:T(8,128)(2,1)}, bf16[1024,512]{1,0:T(8,128)(2,1)}, u32[]{:S(2)}, u32[]{:S(2)}) %collective-permute-start.40) | collective-permute-done | bytes 1048608 | tf_op jit(solution)/shard_map/ppermute | solution.py:51
  362.4 16.1 %collective-permute-done.50.refs_4_ = bf16[256,1024]{1,0:T(8,128)(2,1)} collective-permute-done((bf16[256,1024]{1,0:T(8,128)(2,1)}, bf16[256,1024]{1,0:T(8,128)(2,1)}, u32[]{:S(2)}, u32[]{:S(2)}) %collective-permute-start.50) | collective-permute-done | bytes 524320 | tf_op jit(solution)/shard_map/ppermute | solution.py:38
  380.1 8.7 %strip_rows.5 = (bf16[512,1280]{1,0:T(8,128)(2,1)}, bf16[256,1280]{1,0:T(8,128)(2,1)}, bf16[256,1280]{1,0:T(8,128)(2,1)}) custom-call(s32[2,4]{1,0:T(2,128)} %pad_add_fusion.tbl, bf16[256,2048]{1,0:T(8,128)(2,1)} %multiply_convert_fusion.1.own_ref.refs_0_, bf16[256,2048]{1,0:T(8,128)(2,1)} %collective-permute-done.18.other_ref.refs_1_, ...), custom_call_target="tpu_custom_call" | custom-call | flops 2100000000 | tf_op jit(solution)/shard_map/strip_rows/pallas_call | solution.py:557
  410.0 6.5 %collective-permute-done.48 = bf16[512,512]{1,0:T(8,128)(2,1)} collective-permute-done((bf16[512,512]{1,0:T(8,128)(2,1)}, bf16[512,512]{1,0:T(8,128)(2,1)}, u32[]{:S(2)}, u32[]{:S(2)}) %collective-permute-start.48) | collective-permute-done | bytes 524320 | tf_op jit(solution)/shard_map/ppermute | solution.py:51
  419.2 6.1 %project.5 = (bf16[256,2048]{1,0:T(8,128)(2,1)}, bf16[256,2048]{1,0:T(8,128)(2,1)}) custom-call(bf16[512,512]{1,0:T(8,128)(2,1)} %get-tuple-element.193.refs_0_.refs_3_, bf16[2048,512]{1,0:T(8,128)(2,1)} %refs_1_.5, bf16[512,256]{1,0:T(8,128)(2,1)} %get-tuple-element.184.refs_2_.refs_3_, bf16[2048,256]{1,0:T(8,128)(2,1)} %refs_3_.1, ...), custom_call_target="tpu_custom_call" | custom-call | flops 1800000000 | tf_op jit(solution)/shard_map/project/pallas_call | solution.py:349
  425.3 30.4 %collective-permute-done.61 = bf16[512,512]{1,0:T(8,128)(2,1)S(1)} collective-permute-done((bf16[512,512]{1,0:T(8,128)(2,1)}, bf16[512,512]{1,0:T(8,128)(2,1)S(1)}, u32[]{:S(2)}, u32[]{:S(2)}) %collective-permute-start.61) | collective-permute-done | bytes 524320 | tf_op jit(solution)/shard_map/ppermute | solution.py:51
  458.8 6.1 %strip_rows.7 = (bf16[512,512]{1,0:T(8,128)(2,1)}, bf16[256,512]{1,0:T(8,128)(2,1)}, bf16[256,512]{1,0:T(8,128)(2,1)}) custom-call(s32[2,4]{1,0:T(2,128)} %pad_add_fusion.tbl, bf16[512,2048]{1,0:T(8,128)(2,1)} %get-tuple-element.204.x_ref.refs_0_, bf16[256,2048]{1,0:T(8,128)(2,1)} %copy-done, bf16[256,2048]{1,0:T(8,128)(2,1)} %collective-permute-done.22.refs_4_.refs_2_, ...), custom_call_target="tpu_custom_call" | custom-call | flops 1200000000 | tf_op jit(solution)/shard_map/strip_rows/pallas_call | solution.py:557
  465.0 10.8 %collective-permute-done.49 = bf16[256,512]{1,0:T(8,128)(2,1)} collective-permute-done((bf16[256,512]{1,0:T(8,128)(2,1)}, bf16[256,512]{1,0:T(8,128)(2,1)}, u32[]{:S(2)}, u32[]{:S(2)}) %collective-permute-start.49) | collective-permute-done | bytes 262176 | tf_op jit(solution)/shard_map/ppermute | solution.py:51
  481.9 17.5 %collective-permute-done.54 = bf16[512,512]{1,0:T(8,128)(2,1)S(1)} collective-permute-done((bf16[512,512]{1,0:T(8,128)(2,1)}, bf16[512,512]{1,0:T(8,128)(2,1)S(1)}, u32[]{:S(2)}, u32[]{:S(2)}) %collective-permute-start.54) | collective-permute-done | bytes 524320 | tf_op jit(solution)/shard_map/ppermute | solution.py:51
  502.0 20.4 %collective-permute-done.55 = bf16[256,512]{1,0:T(8,128)(2,1)S(1)} collective-permute-done((bf16[256,512]{1,0:T(8,128)(2,1)S(1)}, bf16[256,512]{1,0:T(8,128)(2,1)S(1)}, u32[]{:S(2)}, u32[]{:S(2)}) %collective-permute-start.55) | collective-permute-done | bytes 262176 | tf_op jit(solution)/shard_map/ppermute | solution.py:51
  (321 shorter events, 210.2 us)
Async XLA Ops:
  48.9 53.5 %collective-permute-start.14 = (bf16[256,2048]{1,0:T(8,128)(2,1)}, bf16[256,2048]{1,0:T(8,128)(2,1)S(1)}, u32[]{:S(2)}, u32[]{:S(2)}) collective-permute-start(bf16[256,2048]{1,0:T(8,128)(2,1)} %get-tuple-element.137), channel_id=1, source_target_pairs={{0,4},{4,0},{8,12},{12,8},{16,20},{20,16},{24,28},{28,24},{1,5},{5... | collective-permute-start | bytes 3145736 | tf_op jit(solution)/shard_map/ppermute | solution.py:38
  173.8 33.5 %collective-permute-start.23 = (bf16[256,2048]{1,0:T(8,128)(2,1)}, bf16[256,2048]{1,0:T(8,128)(2,1)}, u32[]{:S(2)}, u32[]{:S(2)}) collective-permute-start(bf16[256,2048]{1,0:T(8,128)(2,1)} %add_convert_fusion.4), channel_id=1, source_target_pairs={{0,2},{1,3},{2,0},{3,1},{4,6},{5,7},{6,4},{7,5},{8,10},{9,11},{10,... | collective-permute-start | bytes 3145736 | tf_op jit(solution)/shard_map/ppermute | solution.py:34
  182.2 33.1 %collective-permute-start.25 = (bf16[512,768]{1,0:T(8,128)(2,1)}, bf16[512,768]{1,0:T(8,128)(2,1)}, u32[]{:S(2)}, u32[]{:S(2)}) collective-permute-start(bf16[512,768]{1,0:T(8,128)(2,1)} %get-tuple-element.161.gate_a.refs_4_), channel_id=1, source_target_pairs={{0,4},{4,0},{8,12},{12,8},{16,20},{20,16},{24,28},{28,24},{1,5},{5... | collective-permute-start | bytes 2359304 | tf_op jit(solution)/shard_map/ppermute | solution.py:38
  215.8 49.9 %collective-permute-start.37 = (bf16[512,768]{1,0:T(8,128)(2,1)}, bf16[512,768]{1,0:T(8,128)(2,1)}, u32[]{:S(2)}, u32[]{:S(2)}) collective-permute-start(bf16[512,768]{1,0:T(8,128)(2,1)} %get-tuple-element.177.up_a.refs_5_), channel_id=1, source_target_pairs={{0,4},{4,0},{8,12},{12,8},{16,20},{20,16},{24,28},{28,24},{1,5},{5... | collective-permute-start | bytes 2359304 | tf_op jit(solution)/shard_map/ppermute | solution.py:38
  216.1 49.6 %collective-permute-start.36 = (bf16[256,1024]{1,0:T(8,128)(2,1)}, bf16[256,1024]{1,0:T(8,128)(2,1)}, u32[]{:S(2)}, u32[]{:S(2)}) collective-permute-start(bf16[256,1024]{1,0:T(8,128)(2,1)} %collective-permute-done.19.refs_2_), channel_id=1, source_target_pairs={{0,1},{1,0},{2,3},{3,2},{4,5},{5,4},{6,7},{7,6},{8,9},{9,8},{10,11... | collective-permute-start | bytes 1572872 | tf_op jit(solution)/shard_map/ppermute | solution.py:34
  216.1 49.6 %collective-permute-start.34 = (bf16[768,256]{1,0:T(8,128)(2,1)S(1)}, bf16[768,256]{1,0:T(8,128)(2,1)}, u32[]{:S(2)}, u32[]{:S(2)}) collective-permute-start(bf16[768,256]{1,0:T(8,128)(2,1)S(1)} %add_convert_fusion.10), channel_id=1, source_target_pairs={{0,16},{4,20},{8,24},{12,28},{16,0},{20,4},{24,8},{28,12},{1,17},{... | collective-permute-start | bytes 1179656 | tf_op jit(solution)/shard_map/ppermute | solution.py:51
  275.0 40.3 %collective-permute-start.38 = (bf16[512,1536]{1,0:T(8,128)(2,1)}, bf16[512,1536]{1,0:T(8,128)(2,1)S(1)}, u32[]{:S(2)}, u32[]{:S(2)}) collective-permute-start(bf16[512,1536]{1,0:T(8,128)(2,1)} %get-tuple-element.179), channel_id=1, source_target_pairs={{0,8},{4,12},{8,0},{12,4},{16,24},{20,28},{24,16},{28,20},{1,9},{5... | collective-permute-start | bytes 4718600 | tf_op jit(solution)/shard_map/ppermute | solution.py:51
  280.0 36.7 %collective-permute-start.33 = (bf16[1024,512]{1,0:T(8,128)(2,1)}, bf16[1024,512]{1,0:T(8,128)(2,1)S(1)}, u32[]{:S(2)}, u32[]{:S(2)}) collective-permute-start(bf16[1024,512]{1,0:T(8,128)(2,1)} %get-tuple-element.174), channel_id=1, source_target_pairs={{0,4},{4,0},{8,12},{12,8},{16,20},{20,16},{24,28},{28,24},{1,5},{5... | collective-permute-start | bytes 3145736 | tf_op jit(solution)/shard_map/ppermute | solution.py:38
  280.0 36.7 %collective-permute-start.39 = (bf16[512,512]{1,0:T(8,128)(2,1)}, bf16[512,512]{1,0:T(8,128)(2,1)S(1)}, u32[]{:S(2)}, u32[]{:S(2)}) collective-permute-start(bf16[512,512]{1,0:T(8,128)(2,1)} %get-tuple-element.180), channel_id=1, source_target_pairs={{0,4},{4,0},{8,12},{12,8},{16,20},{20,16},{24,28},{28,24},{1,5},{5... | collective-permute-start | bytes 1572872 | tf_op jit(solution)/shard_map/ppermute | solution.py:38
  284.0 46.6 %collective-permute-start.29 = (bf16[256,2048]{1,0:T(8,128)(2,1)S(1)}, bf16[256,2048]{1,0:T(8,128)(2,1)}, u32[]{:S(2)}, u32[]{:S(2)}) collective-permute-start(bf16[256,2048]{1,0:T(8,128)(2,1)S(1)} %add_convert_fusion.3), channel_id=1, source_target_pairs={{0,2},{1,3},{2,0},{3,1},{4,6},{5,7},{6,4},{7,5},{8,10},{9,11},{10,... | collective-permute-start | bytes 3145736 | tf_op jit(solution)/shard_map/ppermute | solution.py:34
  318.1 38.2 %collective-permute-start.40 = (bf16[1024,512]{1,0:T(8,128)(2,1)}, bf16[1024,512]{1,0:T(8,128)(2,1)}, u32[]{:S(2)}, u32[]{:S(2)}) collective-permute-start(bf16[1024,512]{1,0:T(8,128)(2,1)} %add_convert_fusion.1), channel_id=1, source_target_pairs={{0,8},{4,12},{8,0},{12,4},{16,24},{20,28},{24,16},{28,20},{1,9},{5... | collective-permute-start | bytes 3145736 | tf_op jit(solution)/shard_map/ppermute | solution.py:51
  324.1 37.2 %collective-permute-start.45 = (bf16[512,640]{1,0:T(8,128)(2,1)}, bf16[512,640]{1,0:T(8,128)(2,1)}, u32[]{:S(2)}, u32[]{:S(2)}) collective-permute-start(bf16[512,640]{1,0:T(8,128)(2,1)} %get-tuple-element.189.gate_b.refs_4_), channel_id=1, source_target_pairs={{0,4},{4,0},{8,12},{12,8},{16,20},{20,16},{24,28},{28,24},{1,5},{5... | collective-permute-start | bytes 1966088 | tf_op jit(solution)/shard_map/ppermute | solution.py:38
  324.1 54.4 %collective-permute-start.46 = (bf16[512,640]{1,0:T(8,128)(2,1)}, bf16[512,640]{1,0:T(8,128)(2,1)}, u32[]{:S(2)}, u32[]{:S(2)}) collective-permute-start(bf16[512,640]{1,0:T(8,128)(2,1)} %get-tuple-element.190.up_b.refs_5_), channel_id=1, source_target_pairs={{0,4},{4,0},{8,12},{12,8},{16,20},{20,16},{24,28},{28,24},{1,5},{5... | collective-permute-start | bytes 1966088 | tf_op jit(solution)/shard_map/ppermute | solution.py:38
  329.0 66.5 %collective-permute-start.56 = (bf16[256,1536]{1,0:T(8,128)(2,1)}, bf16[256,1536]{1,0:T(8,128)(2,1)}, u32[]{:S(2)}, u32[]{:S(2)}) collective-permute-start(bf16[256,1536]{1,0:T(8,128)(2,1)} %add_convert_fusion.6), channel_id=1, source_target_pairs={{0,16},{4,20},{8,24},{12,28},{16,0},{20,4},{24,8},{28,12},{1,17},{... | collective-permute-start | bytes 2359304 | tf_op jit(solution)/shard_map/ppermute | solution.py:51
  330.7 58.1 %collective-permute-start.47 = (bf16[512,512]{1,0:T(8,128)(2,1)}, bf16[512,512]{1,0:T(8,128)(2,1)}, u32[]{:S(2)}, u32[]{:S(2)}) collective-permute-start(bf16[512,512]{1,0:T(8,128)(2,1)} %get-tuple-element.193.refs_0_.refs_3_), channel_id=1, source_target_pairs={{0,4},{4,0},{8,12},{12,8},{16,20},{20,16},{24,28},{28,24},{1,5},{5... | collective-permute-start | bytes 1572872 | tf_op jit(solution)/shard_map/ppermute | solution.py:38
  361.3 44.2 %collective-permute-start.32 = (bf16[512,512]{1,0:T(8,128)(2,1)}, bf16[512,512]{1,0:T(8,128)(2,1)}, u32[]{:S(2)}, u32[]{:S(2)}) collective-permute-start(bf16[512,512]{1,0:T(8,128)(2,1)} %get-tuple-element.172), channel_id=1, source_target_pairs={{0,4},{4,0},{8,12},{12,8},{16,20},{20,16},{24,28},{28,24},{1,5},{5... | collective-permute-start | bytes 1572872 | tf_op jit(solution)/shard_map/ppermute | solution.py:38
  397.4 80.6 %collective-permute-start.57 = (bf16[512,1280]{1,0:T(8,128)(2,1)}, bf16[512,1280]{1,0:T(8,128)(2,1)}, u32[]{:S(2)}, u32[]{:S(2)}) collective-permute-start(bf16[512,1280]{1,0:T(8,128)(2,1)} %get-tuple-element.191), channel_id=1, source_target_pairs={{0,8},{4,12},{8,0},{12,4},{16,24},{20,28},{24,16},{28,20},{1,9},{5... | collective-permute-start | bytes 3932168 | tf_op jit(solution)/shard_map/ppermute | solution.py:51
  403.4 52.3 %collective-permute-start.61 = (bf16[512,512]{1,0:T(8,128)(2,1)}, bf16[512,512]{1,0:T(8,128)(2,1)S(1)}, u32[]{:S(2)}, u32[]{:S(2)}) collective-permute-start(bf16[512,512]{1,0:T(8,128)(2,1)} %get-tuple-element.203), channel_id=1, source_target_pairs={{0,8},{4,12},{8,0},{12,4},{16,24},{20,28},{24,16},{28,20},{1,9},{5... | collective-permute-start | bytes 1572872 | tf_op jit(solution)/shard_map/ppermute | solution.py:51
  405.5 128.7 %collective-permute-start.30 = (bf16[256,2048]{1,0:T(8,128)(2,1)S(1)}, bf16[256,2048]{1,0:T(8,128)(2,1)S(1)}, u32[]{:S(2)}, u32[]{:S(2)}) collective-permute-start(bf16[256,2048]{1,0:T(8,128)(2,1)S(1)} %add_convert_fusion.2), channel_id=1, source_target_pairs={{0,1},{1,0},{2,3},{3,2},{4,5},{5,4},{6,7},{7,6},{8,9},{9,8},{10,11... | collective-permute-start | bytes 3145736 | tf_op jit(solution)/shard_map/ppermute | solution.py:34
  408.3 47.6 %collective-permute-start.52 = (bf16[512,256]{1,0:T(8,128)(2,1)}, bf16[512,256]{1,0:T(8,128)(2,1)S(1)}, u32[]{:S(2)}, u32[]{:S(2)}) collective-permute-start(bf16[512,256]{1,0:T(8,128)(2,1)} %get-tuple-element.184.refs_2_.refs_3_), channel_id=1, source_target_pairs={{0,4},{4,0},{8,12},{12,8},{16,20},{20,16},{24,28},{28,24},{1,5},{5... | collective-permute-start | bytes 786440 | tf_op jit(solution)/shard_map/ppermute | solution.py:38
  416.5 39.5 %collective-permute-start.53 = (bf16[512,256]{1,0:T(8,128)(2,1)}, bf16[512,256]{1,0:T(8,128)(2,1)}, u32[]{:S(2)}, u32[]{:S(2)}) collective-permute-start(bf16[512,256]{1,0:T(8,128)(2,1)} %get-tuple-element.185.refs_4_), channel_id=1, source_target_pairs={{0,4},{4,0},{8,12},{12,8},{16,20},{20,16},{24,28},{28,24},{1,5},{5... | collective-permute-start | bytes 786440 | tf_op jit(solution)/shard_map/ppermute | solution.py:38
  455.9 43.8 %collective-permute-start.42 = (bf16[256,2048]{1,0:T(8,128)(2,1)}, bf16[256,2048]{1,0:T(8,128)(2,1)}, u32[]{:S(2)}, u32[]{:S(2)}) collective-permute-start(bf16[256,2048]{1,0:T(8,128)(2,1)} %get-tuple-element.187), channel_id=1, source_target_pairs={{0,1},{1,0},{2,3},{3,2},{4,5},{5,4},{6,7},{7,6},{8,9},{9,8},{10,11... | collective-permute-start | bytes 3145736 | tf_op jit(solution)/shard_map/ppermute | solution.py:34
  456.0 81.1 %collective-permute-start.62 = (bf16[512,256]{1,0:T(8,128)(2,1)S(1)}, bf16[512,256]{1,0:T(8,128)(2,1)}, u32[]{:S(2)}, u32[]{:S(2)}) collective-permute-start(bf16[512,256]{1,0:T(8,128)(2,1)S(1)} %add_convert_fusion.12), channel_id=1, source_target_pairs={{0,16},{4,20},{8,24},{12,28},{16,0},{20,4},{24,8},{28,12},{1,17},{... | collective-permute-start | bytes 786440 | tf_op jit(solution)/shard_map/ppermute | solution.py:51
  479.4 44.9 %collective-permute-start.58 = (bf16[256,1280]{1,0:T(8,128)(2,1)S(1)}, bf16[256,1280]{1,0:T(8,128)(2,1)S(1)}, u32[]{:S(2)}, u32[]{:S(2)}) collective-permute-start(bf16[256,1280]{1,0:T(8,128)(2,1)S(1)} %add_convert_fusion.7), channel_id=1, source_target_pairs={{0,16},{4,20},{8,24},{12,28},{16,0},{20,4},{24,8},{28,12},{1,17},{... | collective-permute-start | bytes 1966088 | tf_op jit(solution)/shard_map/ppermute | solution.py:51
  (99 other events, 1782.9 us)
where the time goes:
time: 552 us; the launch traced here: 543 us
  waiting for transfers between devices  253 us (46%)
  Pallas kernels  152 us (28%)
  starting transfers between devices  66.8 us (12%)
  other arithmetic  59.4 us (11%)
  local copies, waits for them, and re-layouts  9.83 us (2%)
    ppermute x16, waiting for transfers between devices, wide_flip(): lax.ppermute(value, 'wide', [(w, w ^ 2 << bit) for w in range(lax.axis_si...  159 us
    ppermute x23, waiting for transfers between devices, wide_swap(): lax.ppermute(value, 'wide', [(w, w ^ 1) for w in range(lax.axis_size('wid...  54.3 us
    ppermute x17, waiting for transfers between devices, narrow_swap(): return lax.ppermute(value, 'narrow', pairs)  31 us
    pallas_call x4, Pallas kernels, strip_rows_grad(): pl.pallas_call(functools.partial(strip_rows_kernel, len(left), len(left_n...  29.9 us
    ppermute x16, starting transfers between devices, wide_flip(): lax.ppermute(value, 'wide', [(w, w ^ 2 << bit) for w in range(lax.axis_si...  28.5 us
    ppermute x23, starting transfers between devices, wide_swap(): lax.ppermute(value, 'wide', [(w, w ^ 1) for w in range(lax.axis_size('wid...  24.9 us
    pallas_call x3, Pallas kernels, project(): pl.pallas_call(functools.partial(project_kernel, plan), out_shape=[jax.Sh...  16.8 us
    pallas_call x1, Pallas kernels, attn_bwd(): pl.pallas_call(functools.partial(attn_bwd_kernel, heads, count, groups),...  16.2 us
  transfers between devices with their start and end apart: 63, of which 26 were waited for; matrix products, arithmetic and copies ran while one was open for 10% of the time, Pallas kernels for 27%

commit v1 on v0

--- a/solution.py
+++ b/solution.py
@@ -777,7 +777,7 @@
             if step == 2 and head == 0:
                 input_near, d_dense_strips = done[-2:]
     slots = [n + f for n, f in zip(near, far)]
-    input_near = wide_swap(after(input_near, far[0][-2]))
+    input_near = wide_swap(after(input_near, *slots[0], *slots[-1]))
     mixed, lse = None, []
     for h, held in enumerate(slots):
         mixed, part = attn_fwd(h, meta, query, pos_row, low_row, held, mixed)
@@ -803,9 +803,6 @@
     scale_two = lax.rsqrt(jnp.mean(hidden_one * hidden_one, axis=1, keepdims=True) + EPSILON)
     normed_two = (hidden_one * scale_two * gain_two).astype(BF)
     normed_two_other = narrow_swap(after(normed_two, mixed_near), 1)
-    (normed_two_near,) = pack([normed_two], [[(0, low_rows, 1)]], tbl, strip)
-    normed_two_near = wide_swap(normed_two_near)
-
     hidden = w_gate.shape[1]
     tile = 256
     first_count = 3 * tile
@@ -823,7 +820,7 @@
         hidden - first_count,
         tile,
     )
-    back = back_dense([*dgu_a, dgu_b[0], after(dgu_b[1], normed_two_near)], w_gate, w_up, 512, 0, 1)
+    back = back_dense([*dgu_a, *dgu_b], w_gate, w_up, 512, 0, 1)
     held, got = reduce_narrow((back[0], after(back[1], inner_a_near)))
 
     def halve(parts, axis, hold=None):
@@ -842,9 +839,8 @@
                     ]
                     total = total + (pick[0] if len(pick) == 1 else jnp.concatenate(pick, axis)).astype(F32)
                 sent = total.astype(BF)
-                if hold is not None:
-                    sent = after(sent, hold)
-            received.append(wide_flip(sent, bit))
+            got = wide_flip(sent, bit)
+            received.append(got if hold is None else after(got, hold))
         return received, sent
 
     def close(parts, received, axis):
@@ -867,18 +863,18 @@
         1,
     )
     inner_b_near = wide_swap(inner_b)
-    normed_two_near_other = narrow_swap(after(normed_two_near, held), 1)
     down_a_got, down_a_mid = halve(down_a, 1)
     dgu_a_near = [wide_swap(after(v, inner_b)) for v in dgu_a]
     dense_parts = project(
-        [(after(inner_a, down_a[0]), w_down, 0), (inner_b, w_down, first_count)], "nn", 512, 6
-    )
+        [(after(inner_a, down_a[0], inner_b_near), w_down, 0), (inner_b, w_down, first_count)], "nn", 512, 6
+    )
+    (normed_two_near,) = pack([after(normed_two, dense_parts[0])], [[(0, low_rows, 1)]], tbl, strip)
+    normed_two_near = wide_swap(normed_two_near)
     down_b = strip_columns_grad(
         [after(inner_b, dense_parts[0])], [inner_b_near], [d_dense_strips], near_sides, turns, strip, tile, 4, 1
     )
 
     got = after(got, dense_parts[0], down_b[0])
-    down_b_got, down_b_mid = halve(down_b, 1, got)
     upstream = own_half(cotangent).astype(F32)
     d_hidden = upstream + norm_backward(hidden_one, scale_two, gain_two, total_of(held, got))
     d_attn = (keep_own * d_hidden).astype(BF)
@@ -886,18 +882,20 @@
 
     d_mixed = mixed_grad(d_attn, d_attn_other, w_out)
     d_query, d_near, d_far = attn_bwd(
-        meta, query, pos_row, low_row, lse, mixed, after(d_mixed, down_b_mid), cosine, sine, slots
+        meta, query, pos_row, low_row, lse, mixed, d_mixed, cosine, sine, slots
     )
     held_out, got_out = reduce_narrow((dense_parts[0], after(dense_parts[1], d_mixed)))
     output_own = (hidden_one + keep_own * total_of(held_out, got_out)).astype(BF)
     output = ordered(output_own, narrow_swap(output_own, 1))
 
-    d_far = [wide_swap(v) for v in d_far]
+    down_b_got, down_b_mid = halve(down_b, 1, d_query)
+    normed_two_near_other = narrow_swap(after(normed_two_near, d_query), 1)
     normed_two_sides = [normed_two_near, normed_two_near_other]
     gate_up_a = strip_rows_grad(
-        [after(normed_two, d_query, down_a_got[-1], down_b_got[-1]), normed_two_other], normed_two_sides, dgu_a, dgu_a_near, tbl, strip, 8
-    )
-    gate_up_a_got, gate_up_a_mid = halve(gate_up_a, 0, d_far[1])
+        [after(normed_two, d_query, down_b_mid), normed_two_other], normed_two_sides, dgu_a, dgu_a_near, tbl, strip, 8
+    )
+    gate_up_a_got, gate_up_a_mid = halve(gate_up_a, 0)
+    d_far = [wide_swap(v) for v in d_far]
     d_far[0] = after(d_far[0], gate_up_a_mid)
     pairs = [
         (n.astype(F32) + f.astype(F32)).astype(BF) for n, f in zip(d_near[:-1], d_far[:-1])
@@ -924,11 +922,10 @@
         strip,
     )
     d_attn_near = wide_swap(after(d_attn_near, pairs[0]))
-    d_attn_near_other = narrow_swap(d_attn_near, 1)
+    d_attn_near_other = narrow_swap(after(d_attn_near, gate_up_b[0]), 1)
     query_part = strip_rows_grad(
         [after(normed_one, gate_up_b[0])], near_sides, [d_query], [d_query_near], tbl, strip, 4
     )
-    query_got, query_mid = halve(query_part, 0)
     out_part = strip_columns_grad(
         [after(mixed, query_part[0])],
         [mixed_near],
@@ -939,7 +936,6 @@
         tile,
         4,
     )
-    out_got, out_mid = halve(out_part, 1)
 
     kv_width = w_key.shape[1]
     held, got = reduce_narrow(
@@ -963,6 +959,9 @@
         4,
     )
     kv_part_got, _ = halve(kv_part, 0)
+    query_got, query_mid = halve(query_part, 0, kv_part[0])
+    out_got, out_mid = halve(out_part, 1, kv_part[0])
+    kv_part_got[-1] = after(kv_part_got[-1], grad_own, output)
     grad_kv = close(kv_part, kv_part_got, 0)
     grad_down_a = close(down_a, down_a_got, 1)
     grad_down_b = close(down_b, down_b_got, 1)

time: 552 us -> 507 us (0.918)
  waiting for transfers between devices: 253 us -> 228 us
  Pallas kernels: 152 us -> 146 us
    ppermute x23, waiting for transfers between devices: 54.3 us -> 39.7 us  [wide_swap(): lax.ppermute(value, 'wide', [(w, w ^ 1) for w in range(lax.axis_size('wid...]
    ppermute x16, waiting for transfers between devices: 159 us -> 147 us  [wide_flip(): lax.ppermute(value, 'wide', [(w, w ^ 2 << bit) for w in range(lax.axis_si...]
    ppermute x16, starting transfers between devices: 28.5 us -> 19.3 us  [wide_flip(): lax.ppermute(value, 'wide', [(w, w ^ 2 << bit) for w in range(lax.axis_si...]
  transfers between devices with their start and end apart: 63 -> 63, of which waited for: 26 -> 30; matrix products, arithmetic and copies ran while one was open for 10% -> 11% of each run, Pallas kernels for 27% -> 26%
where the time goes in v1:
time: 507 us; the launch traced here: 503 us
  waiting for transfers between devices  228 us (45%)
  Pallas kernels  146 us (29%)
  starting transfers between devices  61.4 us (12%)
  other arithmetic  56.6 us (11%)
  local copies, waits for them, and re-layouts  9.87 us (2%)
    ppermute x16, waiting for transfers between devices, wide_flip(): lax.ppermute(value, 'wide', [(w, w ^ 2 << bit) for w in range(lax.axis_si...  147 us
    ppermute x23, waiting for transfers between devices, wide_swap(): lax.ppermute(value, 'wide', [(w, w ^ 1) for w in range(lax.axis_size('wid...  39.7 us
    ppermute x17, waiting for transfers between devices, narrow_swap(): return lax.ppermute(value, 'narrow', pairs)  32.1 us
    pallas_call x4, Pallas kernels, strip_rows_grad(): pl.pallas_call(functools.partial(strip_rows_kernel, len(left), len(left_n...  29.4 us
    ppermute x23, starting transfers between devices, wide_swap(): lax.ppermute(value, 'wide', [(w, w ^ 1) for w in range(lax.axis_size('wid...  27.2 us
    ppermute x16, starting transfers between devices, wide_flip(): lax.ppermute(value, 'wide', [(w, w ^ 2 << bit) for w in range(lax.axis_si...  19.3 us
    pallas_call x3, Pallas kernels, project(): pl.pallas_call(functools.partial(project_kernel, plan), out_shape=[jax.Sh...  17 us
    pallas_call x2, Pallas kernels, gated(): pl.pallas_call(gated_kernel, out_shape=[jax.ShapeDtypeStruct((2 * half, c...  16 us
  transfers between devices with their start and end apart: 63, of which 30 were waited for; matrix products, arithmetic and copies ran while one was open for 11% of the time, Pallas kernels for 26%

profile of v1, /device:TPU:0, one launch (start us, length us, event | category | flops | bytes accessed | tf_op | source)
XLA Modules:
  0.0 503.3 jit_solution(18354360708801460816)
XLA Ops:
  29.7 8.5 %inner_grad.1.di_ref = f32[512,1408]{1,0:T(8,128)} custom-call(bf16[512,2048]{1,0:T(8,128)(2,1)} %maximum_select_fusion.x_ref.refs_1_, bf16[1408,2048]{1,0:T(8,128)(2,1)} %refs_1_.4), custom_call_target="tpu_custom_call" | custom-call | flops 2400000000 | tf_op jit(solution)/shard_map/inner_grad/pallas_call | solution.py:450
  65.8 5.6 %attn_fwd.3 = (bf16[512,512]{1,0:T(8,128)(2,1)}, f32[2,512]{1,0:T(2,128)}) custom-call(s32[24]{0:T(128)} %pad_add_fusion.2.refs_0_, bf16[512,512]{1,0:T(8,128)(2,1)} %query_proj.1.refs_1_, s32[1,512]{1,0:T(1,128)} %bitcast.33, s32[1,512]{1,0:T(1,128)} %bitcast.30, ...), custom_call_target="tpu_custom_call", output_to_operand_aliasing={{0}: (12, {})} | custom-call | flops 1000000000 | tf_op jit(solution)/shard_map/attn_fwd/pallas_call | solution.py:200
  75.2 6.1 %collective-permute-done.14.refs_3_.refs_1_ = bf16[256,2048]{1,0:T(8,128)(2,1)S(1)} collective-permute-done((bf16[256,2048]{1,0:T(8,128)(2,1)}, bf16[256,2048]{1,0:T(8,128)(2,1)S(1)}, u32[]{:S(2)}, u32[]{:S(2)}) %collective-permute-start.14) | collective-permute-done | bytes 1048608 | tf_op jit(solution)/shard_map/ppermute | solution.py:38
  88.3 22.7 %collective-permute-done.16 = bf16[256,2048]{1,0:T(8,128)(2,1)S(1)} collective-permute-done((bf16[256,2048]{1,0:T(8,128)(2,1)S(1)}, bf16[256,2048]{1,0:T(8,128)(2,1)S(1)}, u32[]{:S(2)}, u32[]{:S(2)}) %collective-permute-start.16) | collective-permute-done | bytes 1048608 | tf_op jit(solution)/shard_map/ppermute | solution.py:34
  116.3 8.2 %gated.2 = (bf16[512,768]{1,0:T(8,128)(2,1)}, bf16[512,768]{1,0:T(8,128)(2,1)}, bf16[512,768]{1,0:T(8,128)(2,1)}) custom-call(bf16[256,2048]{1,0:T(8,128)(2,1)} %copy-done.3, bf16[256,2048]{1,0:T(8,128)(2,1)} %collective-permute-done.18.other_ref.refs_1_, bf16[2048,1408]{1,0:T(8,128)(2,1)} %wg_ref.5, bf16[2048,1408]{1,0:T(8,128)(2,1)} %wu_ref.5, ...), custom_call_target="tpu_custom_call" | custom-call | flops 2249999872 | tf_op jit(solution)/shard_map/gated/pallas_call | solution.py:409
  125.4 7.7 %gated.3 = (bf16[512,640]{1,0:T(8,128)(2,1)}, bf16[512,640]{1,0:T(8,128)(2,1)}, bf16[512,640]{1,0:T(8,128)(2,1)}) custom-call(bf16[256,2048]{1,0:T(8,128)(2,1)} %copy-done.3, bf16[256,2048]{1,0:T(8,128)(2,1)} %collective-permute-done.18.other_ref.refs_1_, bf16[2048,1408]{1,0:T(8,128)(2,1)} %wg_ref.5, bf16[2048,1408]{1,0:T(8,128)(2,1)} %wu_ref.5, ...), custom_call_target="tpu_custom_call" | custom-call | flops 2249999872 | tf_op jit(solution)/shard_map/gated/pallas_call | solution.py:409
  133.2 10.8 %back_dense.1 = (bf16[256,2048]{1,0:T(8,128)(2,1)}, bf16[256,2048]{1,0:T(8,128)(2,1)}) custom-call(bf16[512,768]{1,0:T(8,128)(2,1)} %get-tuple-element.165.gate_a.refs_4_, bf16[512,768]{1,0:T(8,128)(2,1)} %get-tuple-element.181.up_a.refs_5_, bf16[512,640]{1,0:T(8,128)(2,1)} %get-tuple-element.192.gate_b.refs_4_, ...), custom_call_target="tpu_custom_call" | custom-call | flops 3300000000 | tf_op jit(solution)/shard_map/back_dense/pallas_call | solution.py:377
  162.3 7.1 %project.4 = (bf16[256,2048]{1,0:T(8,128)(2,1)}, bf16[256,2048]{1,0:T(8,128)(2,1)}) custom-call(bf16[512,768]{1,0:T(8,128)(2,1)} %get-tuple-element.159.refs_0_, bf16[1408,2048]{1,0:T(8,128)(2,1)} %refs_1_.4, bf16[512,640]{1,0:T(8,128)(2,1)} %get-tuple-element.162.refs_2_.refs_0_), custom_call_target="tpu_custom_call" | custom-call | flops 1800000000 | tf_op jit(solution)/shard_map/project/pallas_call | solution.py:349
  196.7 12.7 %attn_bwd.1 = (bf16[512,512]{1,0:T(8,128)(2,1)}, bf16[1024,512]{1,0:T(8,128)(2,1)}, bf16[512,512]{1,0:T(8,128)(2,1)}, bf16[512,512]{1,0:T(8,128)(2,1)}, bf16[102...) custom-call(s32[24]{0:T(128)} %pad_add_fusion.2.refs_0_, ...), custom_call_target="tpu_custom_call" | custom-call | flops 2000000000 | tf_op jit(solution)/shard_map/attn_bwd/pallas_call | solution.py:290
  211.8 7.9 %collective-permute-done.35.refs_7_ = bf16[512,768]{1,0:T(8,128)(2,1)} collective-permute-done((bf16[512,768]{1,0:T(8,128)(2,1)}, bf16[512,768]{1,0:T(8,128)(2,1)}, u32[]{:S(2)}, u32[]{:S(2)}) %collective-permute-start.35) | collective-permute-done | bytes 786464 | tf_op jit(solution)/shard_map/ppermute | solution.py:38
  219.7 9.0 %strip_rows.4 = (bf16[512,1536]{1,0:T(8,128)(2,1)}, bf16[256,1536]{1,0:T(8,128)(2,1)}, bf16[256,1536]{1,0:T(8,128)(2,1)}) custom-call(s32[2,4]{1,0:T(2,128)} %pad_add_fusion.tbl, bf16[256,2048]{1,0:T(8,128)(2,1)} %copy-done.3, bf16[256,2048]{1,0:T(8,128)(2,1)} %collective-permute-done.18.other_ref.refs_1_, ...), custom_call_target="tpu_custom_call" | custom-call | flops 2400000000 | tf_op jit(solution)/shard_map/strip_rows/pallas_call | solution.py:557
  233.5 40.5 %collective-permute-done.61 = bf16[768,256]{1,0:T(8,128)(2,1)} collective-permute-done((bf16[768,256]{1,0:T(8,128)(2,1)S(1)}, bf16[768,256]{1,0:T(8,128)(2,1)}, u32[]{:S(2)}, u32[]{:S(2)}) %collective-permute-start.61) | collective-permute-done | bytes 393248 | tf_op jit(solution)/shard_map/ppermute | solution.py:51
  276.2 5.7 %collective-permute-start.31 = (bf16[1024,512]{1,0:T(8,128)(2,1)}, bf16[1024,512]{1,0:T(8,128)(2,1)}, u32[]{:S(2)}, u32[]{:S(2)}) collective-permute-start(bf16[1024,512]{1,0:T(8,128)(2,1)} %get-tuple-element.175), channel_id=1, source_target_pairs={{0,4},{4,0},{8,12},{12,8},{16,20},{20,16},{24,28},{28,24},{1,5},{5... | collective-permute-start | bytes 3145736 | tf_op jit(solution)/shard_map/ppermute | solution.py:38
  295.0 11.2 %collective-permute-done.31 = bf16[1024,512]{1,0:T(8,128)(2,1)} collective-permute-done((bf16[1024,512]{1,0:T(8,128)(2,1)}, bf16[1024,512]{1,0:T(8,128)(2,1)}, u32[]{:S(2)}, u32[]{:S(2)}) %collective-permute-start.31) | collective-permute-done | bytes 1048608 | tf_op jit(solution)/shard_map/ppermute | solution.py:38
  317.4 17.5 %collective-permute-done.54 = bf16[256,1536]{1,0:T(8,128)(2,1)S(1)} collective-permute-done((bf16[256,1536]{1,0:T(8,128)(2,1)S(1)}, bf16[256,1536]{1,0:T(8,128)(2,1)S(1)}, u32[]{:S(2)}, u32[]{:S(2)}) %collective-permute-start.54) | collective-permute-done | bytes 786464 | tf_op jit(solution)/shard_map/ppermute | solution.py:51
  336.9 15.1 %collective-permute-done.37.refs_2_ = bf16[1024,512]{1,0:T(8,128)(2,1)S(1)} collective-permute-done((bf16[1024,512]{1,0:T(8,128)(2,1)S(1)}, bf16[1024,512]{1,0:T(8,128)(2,1)S(1)}, u32[]{:S(2)}, u32[]{:S(2)}) %collective-permute-start.37) | collective-permute-done | bytes 1048608 | tf_op jit(solution)/shard_map/ppermute | solution.py:51
  356.0 8.7 %strip_rows.5 = (bf16[512,1280]{1,0:T(8,128)(2,1)}, bf16[256,1280]{1,0:T(8,128)(2,1)}, bf16[256,1280]{1,0:T(8,128)(2,1)}) custom-call(s32[2,4]{1,0:T(2,128)} %pad_add_fusion.tbl, bf16[256,2048]{1,0:T(8,128)(2,1)} %copy-done.3, bf16[256,2048]{1,0:T(8,128)(2,1)} %collective-permute-done.18.other_ref.refs_1_, ...), custom_call_target="tpu_custom_call" | custom-call | flops 2100000000 | tf_op jit(solution)/shard_map/strip_rows/pallas_call | solution.py:557
  367.8 5.8 %strip_rows.6 = (bf16[512,512]{1,0:T(8,128)(2,1)}, bf16[256,512]{1,0:T(8,128)(2,1)}, bf16[256,512]{1,0:T(8,128)(2,1)}) custom-call(s32[2,4]{1,0:T(2,128)} %pad_add_fusion.tbl, bf16[512,2048]{1,0:T(8,128)(2,1)} %get-tuple-element.207.x_ref.refs_0_, bf16[256,2048]{1,0:T(8,128)(2,1)} %copy-done, bf16[256,2048]{1,0:T(8,128)(2,1)} %collective-permute-done.21.refs_4_.refs_2_, ...), custom_call_target="tpu_custom_call" | custom-call | flops 1200000000 | tf_op jit(solution)/shard_map/strip_rows/pallas_call | solution.py:557
  394.9 5.8 %strip_rows.7 = (bf16[512,512]{1,0:T(8,128)(2,1)}, bf16[256,512]{1,0:T(8,128)(2,1)}, bf16[256,512]{1,0:T(8,128)(2,1)}) custom-call(s32[2,4]{1,0:T(2,128)} %pad_add_fusion.tbl, bf16[512,2048]{1,0:T(8,128)(2,1)} %get-tuple-element.207.x_ref.refs_0_, bf16[256,2048]{1,0:T(8,128)(2,1)} %copy-done, bf16[256,2048]{1,0:T(8,128)(2,1)} %collective-permute-done.21.refs_4_.refs_2_, ...), custom_call_target="tpu_custom_call" | custom-call | flops 1200000000 | tf_op jit(solution)/shard_map/strip_rows/pallas_call | solution.py:557
  400.7 16.6 %collective-permute-done.46 = bf16[512,512]{1,0:T(8,128)(2,1)} collective-permute-done((bf16[512,512]{1,0:T(8,128)(2,1)}, bf16[512,512]{1,0:T(8,128)(2,1)}, u32[]{:S(2)}, u32[]{:S(2)}) %collective-permute-start.46) | collective-permute-done | bytes 524320 | tf_op jit(solution)/shard_map/ppermute | solution.py:51
  418.5 6.3 %project.5 = (bf16[256,2048]{1,0:T(8,128)(2,1)}, bf16[256,2048]{1,0:T(8,128)(2,1)}) custom-call(bf16[512,512]{1,0:T(8,128)(2,1)} %get-tuple-element.196.refs_0_.refs_3_, bf16[2048,512]{1,0:T(8,128)(2,1)} %refs_1_.5, bf16[512,256]{1,0:T(8,128)(2,1)} %get-tuple-element.187.refs_2_.refs_3_, bf16[2048,256]{1,0:T(8,128)(2,1)} %refs_3_.1, ...), custom_call_target="tpu_custom_call" | custom-call | flops 1800000000 | tf_op jit(solution)/shard_map/project/pallas_call | solution.py:349
  425.7 8.4 %collective-permute-done.59 = bf16[512,512]{1,0:T(8,128)(2,1)S(1)} collective-permute-done((bf16[512,512]{1,0:T(8,128)(2,1)}, bf16[512,512]{1,0:T(8,128)(2,1)S(1)}, u32[]{:S(2)}, u32[]{:S(2)}) %collective-permute-start.59) | collective-permute-done | bytes 524320 | tf_op jit(solution)/shard_map/ppermute | solution.py:51
  439.5 9.6 %collective-permute-done.52 = bf16[512,512]{1,0:T(8,128)(2,1)S(1)} collective-permute-done((bf16[512,512]{1,0:T(8,128)(2,1)S(1)}, bf16[512,512]{1,0:T(8,128)(2,1)S(1)}, u32[]{:S(2)}, u32[]{:S(2)}) %collective-permute-start.52) | collective-permute-done | bytes 524320 | tf_op jit(solution)/shard_map/ppermute | solution.py:51
  450.1 33.5 %collective-permute-done.56 = bf16[256,1280]{1,0:T(8,128)(2,1)S(1)} collective-permute-done((bf16[256,1280]{1,0:T(8,128)(2,1)S(1)}, bf16[256,1280]{1,0:T(8,128)(2,1)S(1)}, u32[]{:S(2)}, u32[]{:S(2)}) %collective-permute-start.56) | collective-permute-done | bytes 655392 | tf_op jit(solution)/shard_map/ppermute | solution.py:51
  (319 shorter events, 210.3 us)
Async XLA Ops:
  85.8 25.3 %collective-permute-start.16 = (bf16[256,2048]{1,0:T(8,128)(2,1)S(1)}, bf16[256,2048]{1,0:T(8,128)(2,1)S(1)}, u32[]{:S(2)}, u32[]{:S(2)}) collective-permute-start(bf16[256,2048]{1,0:T(8,128)(2,1)S(1)} %add_convert_fusion.5), channel_id=1, source_target_pairs={{0,2},{1,3},{2,0},{3,1},{4,6},{5,7},{6,4},{7,5},{8,10},{9,11},{10,... | collective-permute-start | bytes 3145736 | tf_op jit(solution)/shard_map/ppermute | solution.py:34
  87.4 25.2 %collective-permute-start.17 = (bf16[512,512]{1,0:T(8,128)(2,1)S(1)}, bf16[512,512]{1,0:T(8,128)(2,1)S(1)}, u32[]{:S(2)}, u32[]{:S(2)}) collective-permute-start(bf16[512,512]{1,0:T(8,128)(2,1)S(1)} %copy-done.44), channel_id=1, source_target_pairs={{0,4},{4,0},{8,12},{12,8},{16,20},{20,16},{24,28},{28,24},{1,5},{5... | collective-permute-start | bytes 1572872 | tf_op jit(solution)/shard_map/ppermute | solution.py:38
  149.9 30.3 %collective-permute-start.23 = (bf16[256,2048]{1,0:T(8,128)(2,1)}, bf16[256,2048]{1,0:T(8,128)(2,1)}, u32[]{:S(2)}, u32[]{:S(2)}) collective-permute-start(bf16[256,2048]{1,0:T(8,128)(2,1)} %add_convert_fusion.4), channel_id=1, source_target_pairs={{0,2},{1,3},{2,0},{3,1},{4,6},{5,7},{6,4},{7,5},{8,10},{9,11},{10,... | collective-permute-start | bytes 3145736 | tf_op jit(solution)/shard_map/ppermute | solution.py:34
  161.0 25.1 %collective-permute-start.24 = (bf16[512,768]{1,0:T(8,128)(2,1)}, bf16[512,768]{1,0:T(8,128)(2,1)}, u32[]{:S(2)}, u32[]{:S(2)}) collective-permute-start(bf16[512,768]{1,0:T(8,128)(2,1)} %get-tuple-element.165.gate_a.refs_4_), channel_id=1, source_target_pairs={{0,4},{4,0},{8,12},{12,8},{16,20},{20,16},{24,28},{28,24},{1,5},{5... | collective-permute-start | bytes 2359304 | tf_op jit(solution)/shard_map/ppermute | solution.py:38
  191.7 28.0 %collective-permute-start.35 = (bf16[512,768]{1,0:T(8,128)(2,1)}, bf16[512,768]{1,0:T(8,128)(2,1)}, u32[]{:S(2)}, u32[]{:S(2)}) collective-permute-start(bf16[512,768]{1,0:T(8,128)(2,1)} %get-tuple-element.181.up_a.refs_5_), channel_id=1, source_target_pairs={{0,4},{4,0},{8,12},{12,8},{16,20},{20,16},{24,28},{28,24},{1,5},{5... | collective-permute-start | bytes 2359304 | tf_op jit(solution)/shard_map/ppermute | solution.py:38
  209.5 76.4 %collective-permute-start.27 = (bf16[256,2048]{1,0:T(8,128)(2,1)}, bf16[256,2048]{1,0:T(8,128)(2,1)}, u32[]{:S(2)}, u32[]{:S(2)}) collective-permute-start(bf16[256,2048]{1,0:T(8,128)(2,1)} %get-tuple-element.168), channel_id=1, source_target_pairs={{0,1},{1,0},{2,3},{3,2},{4,5},{5,4},{6,7},{7,6},{8,9},{9,8},{10,11... | collective-permute-start | bytes 3145736 | tf_op jit(solution)/shard_map/ppermute | solution.py:34
  228.7 64.6 %collective-permute-start.36 = (bf16[512,1536]{1,0:T(8,128)(2,1)}, bf16[512,1536]{1,0:T(8,128)(2,1)}, u32[]{:S(2)}, u32[]{:S(2)}) collective-permute-start(bf16[512,1536]{1,0:T(8,128)(2,1)} %get-tuple-element.183), channel_id=1, source_target_pairs={{0,8},{4,12},{8,0},{12,4},{16,24},{20,28},{24,16},{28,20},{1,9},{5... | collective-permute-start | bytes 4718600 | tf_op jit(solution)/shard_map/ppermute | solution.py:51
  230.6 43.4 %collective-permute-start.61 = (bf16[768,256]{1,0:T(8,128)(2,1)S(1)}, bf16[768,256]{1,0:T(8,128)(2,1)}, u32[]{:S(2)}, u32[]{:S(2)}) collective-permute-start(bf16[768,256]{1,0:T(8,128)(2,1)S(1)} %add_convert_fusion.10), channel_id=1, source_target_pairs={{0,16},{4,20},{8,24},{12,28},{16,0},{20,4},{24,8},{28,12},{1,17},{... | collective-permute-start | bytes 1179656 | tf_op jit(solution)/shard_map/ppermute | solution.py:51
  230.6 51.3 %collective-permute-start.62 = (bf16[640,256]{1,0:T(8,128)(2,1)}, bf16[640,256]{1,0:T(8,128)(2,1)}, u32[]{:S(2)}, u32[]{:S(2)}) collective-permute-start(bf16[640,256]{1,0:T(8,128)(2,1)} %add_convert_fusion.11), channel_id=1, source_target_pairs={{0,16},{4,20},{8,24},{12,28},{16,0},{20,4},{24,8},{28,12},{1,17},{... | collective-permute-start | bytes 983048 | tf_op jit(solution)/shard_map/ppermute | solution.py:51
  276.2 30.0 %collective-permute-start.31 = (bf16[1024,512]{1,0:T(8,128)(2,1)}, bf16[1024,512]{1,0:T(8,128)(2,1)}, u32[]{:S(2)}, u32[]{:S(2)}) collective-permute-start(bf16[1024,512]{1,0:T(8,128)(2,1)} %get-tuple-element.175), channel_id=1, source_target_pairs={{0,4},{4,0},{8,12},{12,8},{16,20},{20,16},{24,28},{28,24},{1,5},{5... | collective-permute-start | bytes 3145736 | tf_op jit(solution)/shard_map/ppermute | solution.py:38
  281.9 35.6 %collective-permute-start.38 = (bf16[512,512]{1,0:T(8,128)(2,1)}, bf16[512,512]{1,0:T(8,128)(2,1)}, u32[]{:S(2)}, u32[]{:S(2)}) collective-permute-start(bf16[512,512]{1,0:T(8,128)(2,1)} %get-tuple-element.186), channel_id=1, source_target_pairs={{0,4},{4,0},{8,12},{12,8},{16,20},{20,16},{24,28},{28,24},{1,5},{5... | collective-permute-start | bytes 1572872 | tf_op jit(solution)/shard_map/ppermute | solution.py:38
  281.9 73.1 %collective-permute-start.43 = (bf16[512,640]{1,0:T(8,128)(2,1)}, bf16[512,640]{1,0:T(8,128)(2,1)}, u32[]{:S(2)}, u32[]{:S(2)}) collective-permute-start(bf16[512,640]{1,0:T(8,128)(2,1)} %get-tuple-element.192.gate_b.refs_4_), channel_id=1, source_target_pairs={{0,4},{4,0},{8,12},{12,8},{16,20},{20,16},{24,28},{28,24},{1,5},{5... | collective-permute-start | bytes 1966088 | tf_op jit(solution)/shard_map/ppermute | solution.py:38
  293.3 62.7 %collective-permute-start.44 = (bf16[512,640]{1,0:T(8,128)(2,1)}, bf16[512,640]{1,0:T(8,128)(2,1)}, u32[]{:S(2)}, u32[]{:S(2)}) collective-permute-start(bf16[512,640]{1,0:T(8,128)(2,1)} %get-tuple-element.193.up_b.refs_5_), channel_id=1, source_target_pairs={{0,4},{4,0},{8,12},{12,8},{16,20},{20,16},{24,28},{28,24},{1,5},{5... | collective-permute-start | bytes 1966088 | tf_op jit(solution)/shard_map/ppermute | solution.py:38
  306.2 28.7 %collective-permute-start.54 = (bf16[256,1536]{1,0:T(8,128)(2,1)S(1)}, bf16[256,1536]{1,0:T(8,128)(2,1)S(1)}, u32[]{:S(2)}, u32[]{:S(2)}) collective-permute-start(bf16[256,1536]{1,0:T(8,128)(2,1)S(1)} %add_convert_fusion.6), channel_id=1, source_target_pairs={{0,16},{4,20},{8,24},{12,28},{16,0},{20,4},{24,8},{28,12},{1,17},{... | collective-permute-start | bytes 2359304 | tf_op jit(solution)/shard_map/ppermute | solution.py:51
  312.0 39.9 %collective-permute-start.37 = (bf16[1024,512]{1,0:T(8,128)(2,1)S(1)}, bf16[1024,512]{1,0:T(8,128)(2,1)S(1)}, u32[]{:S(2)}, u32[]{:S(2)}) collective-permute-start(bf16[1024,512]{1,0:T(8,128)(2,1)S(1)} %add_convert_fusion.1), channel_id=1, source_target_pairs={{0,8},{4,12},{8,0},{12,4},{16,24},{20,28},{24,16},{28,20},{1,9},{5... | collective-permute-start | bytes 3145736 | tf_op jit(solution)/shard_map/ppermute | solution.py:51
  317.4 64.6 %collective-permute-start.29 = (bf16[256,2048]{1,0:T(8,128)(2,1)S(1)}, bf16[256,2048]{1,0:T(8,128)(2,1)}, u32[]{:S(2)}, u32[]{:S(2)}) collective-permute-start(bf16[256,2048]{1,0:T(8,128)(2,1)S(1)} %add_convert_fusion.2), channel_id=1, source_target_pairs={{0,1},{1,0},{2,3},{3,2},{4,5},{5,4},{6,7},{7,6},{8,9},{9,8},{10,11... | collective-permute-start | bytes 3145736 | tf_op jit(solution)/shard_map/ppermute | solution.py:34
  334.9 29.8 %collective-permute-start.47 = (bf16[256,1024]{1,0:T(8,128)(2,1)}, bf16[256,1024]{1,0:T(8,128)(2,1)}, u32[]{:S(2)}, u32[]{:S(2)}) collective-permute-start(bf16[256,1024]{1,0:T(8,128)(2,1)} %get-tuple-element.204), channel_id=1, source_target_pairs={{0,4},{4,0},{8,12},{12,8},{16,20},{20,16},{24,28},{28,24},{1,5},{5... | collective-permute-start | bytes 1572872 | tf_op jit(solution)/shard_map/ppermute | solution.py:38
  367.8 68.5 %collective-permute-start.55 = (bf16[512,1280]{1,0:T(8,128)(2,1)}, bf16[512,1280]{1,0:T(8,128)(2,1)S(1)}, u32[]{:S(2)}, u32[]{:S(2)}) collective-permute-start(bf16[512,1280]{1,0:T(8,128)(2,1)} %get-tuple-element.194), channel_id=1, source_target_pairs={{0,8},{4,12},{8,0},{12,4},{16,24},{20,28},{24,16},{28,20},{1,9},{5... | collective-permute-start | bytes 3932168 | tf_op jit(solution)/shard_map/ppermute | solution.py:51
  376.8 40.6 %collective-permute-start.46 = (bf16[512,512]{1,0:T(8,128)(2,1)}, bf16[512,512]{1,0:T(8,128)(2,1)}, u32[]{:S(2)}, u32[]{:S(2)}) collective-permute-start(bf16[512,512]{1,0:T(8,128)(2,1)} %get-tuple-element.198), channel_id=1, source_target_pairs={{0,8},{4,12},{8,0},{12,4},{16,24},{20,28},{24,16},{28,20},{1,9},{5... | collective-permute-start | bytes 1572872 | tf_op jit(solution)/shard_map/ppermute | solution.py:51
  390.7 43.4 %collective-permute-start.59 = (bf16[512,512]{1,0:T(8,128)(2,1)}, bf16[512,512]{1,0:T(8,128)(2,1)S(1)}, u32[]{:S(2)}, u32[]{:S(2)}) collective-permute-start(bf16[512,512]{1,0:T(8,128)(2,1)} %get-tuple-element.206), channel_id=1, source_target_pairs={{0,8},{4,12},{8,0},{12,4},{16,24},{20,28},{24,16},{28,20},{1,9},{5... | collective-permute-start | bytes 1572872 | tf_op jit(solution)/shard_map/ppermute | solution.py:51
  434.2 62.0 %collective-permute-start.60 = (bf16[512,256]{1,0:T(8,128)(2,1)S(1)}, bf16[512,256]{1,0:T(8,128)(2,1)S(1)}, u32[]{:S(2)}, u32[]{:S(2)}) collective-permute-start(bf16[512,256]{1,0:T(8,128)(2,1)S(1)} %add_convert_fusion.12), channel_id=1, source_target_pairs={{0,16},{4,20},{8,24},{12,28},{16,0},{20,4},{24,8},{28,12},{1,17},{... | collective-permute-start | bytes 786440 | tf_op jit(solution)/shard_map/ppermute | solution.py:51
  436.5 47.1 %collective-permute-start.56 = (bf16[256,1280]{1,0:T(8,128)(2,1)S(1)}, bf16[256,1280]{1,0:T(8,128)(2,1)S(1)}, u32[]{:S(2)}, u32[]{:S(2)}) collective-permute-start(bf16[256,1280]{1,0:T(8,128)(2,1)S(1)} %add_convert_fusion.7), channel_id=1, source_target_pairs={{0,16},{4,20},{8,24},{12,28},{16,0},{20,4},{24,8},{28,12},{1,17},{... | collective-permute-start | bytes 1966088 | tf_op jit(solution)/shard_map/ppermute | solution.py:51
  449.2 43.2 %collective-permute-start.53 = (bf16[256,512]{1,0:T(8,128)(2,1)S(1)}, bf16[256,512]{1,0:T(8,128)(2,1)S(1)}, u32[]{:S(2)}, u32[]{:S(2)}) collective-permute-start(bf16[256,512]{1,0:T(8,128)(2,1)S(1)} %add_convert_fusion.13), channel_id=1, source_target_pairs={{0,16},{4,20},{8,24},{12,28},{16,0},{20,4},{24,8},{28,12},{1,17},{... | collective-permute-start | bytes 786440 | tf_op jit(solution)/shard_map/ppermute | solution.py:51
  449.6 40.3 %collective-permute-start.41 = (bf16[256,2048]{1,0:T(8,128)(2,1)S(1)}, bf16[256,2048]{1,0:T(8,128)(2,1)S(1)}, u32[]{:S(2)}, u32[]{:S(2)}) collective-permute-start(bf16[256,2048]{1,0:T(8,128)(2,1)S(1)} %add_convert_fusion), channel_id=1, source_target_pairs={{0,2},{1,3},{2,0},{3,1},{4,6},{5,7},{6,4},{7,5},{8,10},{9,11},{10,... | collective-permute-start | bytes 3145736 | tf_op jit(solution)/shard_map/ppermute | solution.py:34
  (98 other events, 1428.1 us)

commit v2 on v1

--- a/solution.py
+++ b/solution.py
@@ -526,10 +526,10 @@
                 column += piece.shape[1]
 
 
-def strip_rows_grad(left, left_near, right, right_near, tbl, strip, micros):
+def strip_rows_grad(left, left_near, right, right_near, tbl, strip, micros, single=False):
     turns = tbl.shape[1]
     columns = sum(r.shape[-1] * (r.shape[0] if r.ndim == 3 else 1) for r in right)
-    spans = stretches(halving(turns))
+    spans = [(k, 1) for k in range(turns)] if single else stretches(halving(turns))
     if strip % 128:
         near = jnp.concatenate(left_near, axis=0)
         mine = jnp.concatenate(left, axis=0)
@@ -730,6 +730,8 @@
     order = np.array([k for stretch in halving(turns) for k in stretch], np.int32)
     turn_row = wide_index // 2 ^ order
     tbl = jnp.stack([2 * turn_row + side, 2 * turn_row + 1 - side]).astype(jnp.int32)
+    round_row = (wide_index // 2 - 1 - jnp.arange(turns, dtype=jnp.int32)) % turns
+    round_tbl = jnp.stack([2 * round_row + side, 2 * round_row + 1 - side]).astype(jnp.int32)
     core_arr = core.astype(jnp.int32)[None]
     normed_one, both = norm_kv(core_arr, tokens, gain_attn[None, :], w_key, w_value, cosine, sine)
     low_rows, all_rows = slice(0, half), slice(0, rows)
@@ -843,6 +845,14 @@
             received.append(got if hold is None else after(got, hold))
         return received, sent
 
+    def ring_sum(parts):
+        carried, first = parts[0], None
+        for part in parts[1:]:
+            total = part.astype(F32) + wide_ring(carried, wide).astype(F32)
+            carried = total.astype(BF)
+            first = carried if first is None else first
+        return total, first
+
     def close(parts, received, axis):
         size = parts[-1].shape[axis]
         total = parts[-1].astype(F32)
@@ -868,7 +878,9 @@
     dense_parts = project(
         [(after(inner_a, down_a[0], inner_b_near), w_down, 0), (inner_b, w_down, first_count)], "nn", 512, 6
     )
-    (normed_two_near,) = pack([after(normed_two, dense_parts[0])], [[(0, low_rows, 1)]], tbl, strip)
+    (normed_two_near,) = pack(
+        [after(normed_two, dense_parts[0])], [[(0, low_rows, 1)]], round_tbl, strip
+    )
     normed_two_near = wide_swap(normed_two_near)
     down_b = strip_columns_grad(
         [after(inner_b, dense_parts[0])], [inner_b_near], [d_dense_strips], near_sides, turns, strip, tile, 4, 1
@@ -882,7 +894,7 @@
 
     d_mixed = mixed_grad(d_attn, d_attn_other, w_out)
     d_query, d_near, d_far = attn_bwd(
-        meta, query, pos_row, low_row, lse, mixed, d_mixed, cosine, sine, slots
+        meta, query, pos_row, low_row, lse, mixed, after(d_mixed, down_a_got[-1]), cosine, sine, slots
     )
     held_out, got_out = reduce_narrow((dense_parts[0], after(dense_parts[1], d_mixed)))
     output_own = (hidden_one + keep_own * total_of(held_out, got_out)).astype(BF)
@@ -892,9 +904,9 @@
     normed_two_near_other = narrow_swap(after(normed_two_near, d_query), 1)
     normed_two_sides = [normed_two_near, normed_two_near_other]
     gate_up_a = strip_rows_grad(
-        [after(normed_two, d_query, down_b_mid), normed_two_other], normed_two_sides, dgu_a, dgu_a_near, tbl, strip, 8
-    )
-    gate_up_a_got, gate_up_a_mid = halve(gate_up_a, 0)
+        [after(normed_two, d_query, down_b_mid), normed_two_other], normed_two_sides, dgu_a, dgu_a_near, round_tbl, strip, 8, True
+    )
+    grad_gate_up_a, gate_up_a_mid = ring_sum(gate_up_a)
     d_far = [wide_swap(v) for v in d_far]
     d_far[0] = after(d_far[0], gate_up_a_mid)
     pairs = [
@@ -909,12 +921,13 @@
         normed_two_sides,
         dgu_b,
         dgu_b_near,
-        tbl,
+        round_tbl,
         strip,
         7,
+        True,
     )
     d_query_near = wide_swap(after(d_query, pairs[0]))
-    gate_up_b_got, gate_up_b_mid = halve(gate_up_b, 0)
+    grad_gate_up_b, gate_up_b_mid = ring_sum(gate_up_b)
     d_attn_near, d_attn_strips, d_attn_other_strips = pack(
         [after(d_attn, gate_up_a[0]), d_attn_other],
         [[(0, low_rows, 1)], [(0, low_rows, 0)], [(1, low_rows, 0)]],
@@ -963,10 +976,9 @@
     out_got, out_mid = halve(out_part, 1, kv_part[0])
     kv_part_got[-1] = after(kv_part_got[-1], grad_own, output)
     grad_kv = close(kv_part, kv_part_got, 0)
+    down_a_got[-1], down_b_got[-1] = after(down_a_got[-1], kv_part[0]), after(down_b_got[-1], kv_part[0])
     grad_down_a = close(down_a, down_a_got, 1)
     grad_down_b = close(down_b, down_b_got, 1)
-    grad_gate_up_a = close(gate_up_a, gate_up_a_got, 0)
-    grad_gate_up_b = close(gate_up_b, gate_up_b_got, 0)
     grad_query = close(query_part, query_got, 0)
     grad_out = close(out_part, out_got, 1)
     grad_key, grad_value = grad_kv[:, :kv_width], grad_kv[:, kv_width:]

time: 507 us -> 491 us (0.968)
  waiting for transfers between devices: 228 us -> 192 us
  starting transfers between devices: 61.4 us -> 72.1 us
  other arithmetic: 56.6 us -> 62.4 us
    ppermute x16 -> x12, waiting for transfers between devices: 147 us -> 74.3 us  [wide_flip(): lax.ppermute(value, 'wide', [(w, w ^ 2 << bit) for w in range(lax.axis_si...]
    ppermute x7 -> x13, waiting for transfers between devices: 9.37 us -> 44.9 us  [wide_ring(): return lax.ppermute(value, 'wide', pairs)]
    ppermute x23, starting transfers between devices: 27.2 us -> 39.1 us  [wide_swap(): lax.ppermute(value, 'wide', [(w, w ^ 1) for w in range(lax.axis_size('wid...]
    ppermute x16 -> x12, starting transfers between devices: 19.3 us -> 10.7 us  [wide_flip(): lax.ppermute(value, 'wide', [(w, w ^ 2 << bit) for w in range(lax.axis_si...]
    ppermute x7 -> x13, starting transfers between devices: 8.66 us -> 17 us  [wide_ring(): return lax.ppermute(value, 'wide', pairs)]
    convert_element_type x0 -> x4, other arithmetic: none -> 6.91 us  [ring_sum(): carried = total.astype(BF)]
  transfers between devices with their start and end apart: 63 -> 65, of which waited for: 30 -> 30; matrix products, arithmetic and copies ran while one was open for 11% -> 12% of each run, Pallas kernels for 26% -> 26%
where the time goes in v2:
time: 491 us; the launch traced here: 483 us
  waiting for transfers between devices  192 us (39%)
  Pallas kernels  147 us (30%)
  starting transfers between devices  72.1 us (15%)
  other arithmetic  62.4 us (13%)
  local copies, waits for them, and re-layouts  7.45 us (2%)
    ppermute x12, waiting for transfers between devices, wide_flip(): lax.ppermute(value, 'wide', [(w, w ^ 2 << bit) for w in range(lax.axis_si...  74.3 us
    ppermute x13, waiting for transfers between devices, wide_ring(): return lax.ppermute(value, 'wide', pairs)  44.9 us
    ppermute x23, waiting for transfers between devices, wide_swap(): lax.ppermute(value, 'wide', [(w, w ^ 1) for w in range(lax.axis_size('wid...  43 us
    ppermute x23, starting transfers between devices, wide_swap(): lax.ppermute(value, 'wide', [(w, w ^ 1) for w in range(lax.axis_size('wid...  39.1 us
    pallas_call x4, Pallas kernels, strip_rows_grad(): pl.pallas_call(functools.partial(strip_rows_kernel, len(left), len(left_n...  29.5 us
    ppermute x17, waiting for transfers between devices, narrow_swap(): return lax.ppermute(value, 'narrow', pairs)  29.3 us
    ppermute x13, starting transfers between devices, wide_ring(): return lax.ppermute(value, 'wide', pairs)  17 us
    pallas_call x3, Pallas kernels, project(): pl.pallas_call(functools.partial(project_kernel, plan), out_shape=[jax.Sh...  16.8 us
  transfers between devices with their start and end apart: 65, of which 30 were waited for; matrix products, arithmetic and copies ran while one was open for 12% of the time, Pallas kernels for 26%

profile of v2, /device:TPU:0, one launch (start us, length us, event | category | flops | bytes accessed | tf_op | source)
XLA Modules:
  0.0 482.6 jit_solution(6485559013177192405)
XLA Ops:
  29.6 8.5 %inner_grad.1.di_ref = f32[512,1408]{1,0:T(8,128)} custom-call(bf16[512,2048]{1,0:T(8,128)(2,1)} %maximum_select_fusion.x_ref.refs_1_, bf16[1408,2048]{1,0:T(8,128)(2,1)} %refs_1_.4), custom_call_target="tpu_custom_call" | custom-call | flops 2400000000 | tf_op jit(solution)/shard_map/inner_grad/pallas_call | solution.py:450
  60.3 6.0 %attn_fwd.2 = (bf16[512,512]{1,0:T(8,128)(2,1)}, f32[2,512]{1,0:T(2,128)}) custom-call(s32[24]{0:T(128)} %pad_add_fusion.3.refs_0_, bf16[512,512]{1,0:T(8,128)(2,1)} %query_proj.1.refs_1_, s32[1,512]{1,0:T(1,128)} %bitcast.32, s32[1,512]{1,0:T(1,128)} %bitcast.29, bf16[512,256]{1,0:T(8,128)(2,1)} %get-tuple-element.123.refs_4_.refs_10_, ...), custom_call_target="tpu_custom_call" | custom-call | flops 1000000000 | tf_op jit(solution)/shard_map/attn_fwd/pallas_call | solution.py:200
  66.3 6.1 %attn_fwd.3 = (bf16[512,512]{1,0:T(8,128)(2,1)}, f32[2,512]{1,0:T(2,128)}) custom-call(s32[24]{0:T(128)} %pad_add_fusion.3.refs_0_, bf16[512,512]{1,0:T(8,128)(2,1)} %query_proj.1.refs_1_, s32[1,512]{1,0:T(1,128)} %bitcast.33, s32[1,512]{1,0:T(1,128)} %bitcast.30, ...), custom_call_target="tpu_custom_call", output_to_operand_aliasing={{0}: (12, {})} | custom-call | flops 1000000000 | tf_op jit(solution)/shard_map/attn_fwd/pallas_call | solution.py:200
  91.4 19.7 %collective-permute-done.16 = bf16[256,2048]{1,0:T(8,128)(2,1)S(1)} collective-permute-done((bf16[256,2048]{1,0:T(8,128)(2,1)S(1)}, bf16[256,2048]{1,0:T(8,128)(2,1)S(1)}, u32[]{:S(2)}, u32[]{:S(2)}) %collective-permute-start.16) | collective-permute-done | bytes 1048608 | tf_op jit(solution)/shard_map/ppermute | solution.py:34
  116.3 8.3 %gated.2 = (bf16[512,768]{1,0:T(8,128)(2,1)}, bf16[512,768]{1,0:T(8,128)(2,1)}, bf16[512,768]{1,0:T(8,128)(2,1)}) custom-call(bf16[256,2048]{1,0:T(8,128)(2,1)} %copy-done.3, bf16[256,2048]{1,0:T(8,128)(2,1)} %collective-permute-done.18.other_ref.refs_1_, bf16[2048,1408]{1,0:T(8,128)(2,1)} %wg_ref.5, bf16[2048,1408]{1,0:T(8,128)(2,1)} %wu_ref.5, ...), custom_call_target="tpu_custom_call" | custom-call | flops 2249999872 | tf_op jit(solution)/shard_map/gated/pallas_call | solution.py:409
  128.3 7.7 %gated.3 = (bf16[512,640]{1,0:T(8,128)(2,1)}, bf16[512,640]{1,0:T(8,128)(2,1)}, bf16[512,640]{1,0:T(8,128)(2,1)}) custom-call(bf16[256,2048]{1,0:T(8,128)(2,1)} %copy-done.3, bf16[256,2048]{1,0:T(8,128)(2,1)} %collective-permute-done.18.other_ref.refs_1_, bf16[2048,1408]{1,0:T(8,128)(2,1)} %wg_ref.5, bf16[2048,1408]{1,0:T(8,128)(2,1)} %wu_ref.5, ...), custom_call_target="tpu_custom_call" | custom-call | flops 2249999872 | tf_op jit(solution)/shard_map/gated/pallas_call | solution.py:409
  136.0 10.8 %back_dense.1 = (bf16[256,2048]{1,0:T(8,128)(2,1)}, bf16[256,2048]{1,0:T(8,128)(2,1)}) custom-call(bf16[512,768]{1,0:T(8,128)(2,1)} %get-tuple-element.170.gate_a.refs_4_, bf16[512,768]{1,0:T(8,128)(2,1)} %get-tuple-element.187.up_a.refs_5_, bf16[512,640]{1,0:T(8,128)(2,1)} %get-tuple-element.198.gate_b.refs_4_, ...), custom_call_target="tpu_custom_call" | custom-call | flops 3300000000 | tf_op jit(solution)/shard_map/back_dense/pallas_call | solution.py:377
  165.3 7.1 %project.4 = (bf16[256,2048]{1,0:T(8,128)(2,1)}, bf16[256,2048]{1,0:T(8,128)(2,1)}) custom-call(bf16[512,768]{1,0:T(8,128)(2,1)} %get-tuple-element.164.refs_0_, bf16[1408,2048]{1,0:T(8,128)(2,1)} %refs_1_.4, bf16[512,640]{1,0:T(8,128)(2,1)} %get-tuple-element.167.refs_2_.refs_0_), custom_call_target="tpu_custom_call" | custom-call | flops 1800000000 | tf_op jit(solution)/shard_map/project/pallas_call | solution.py:349
  197.1 9.7 %collective-permute-done.30 = bf16[768,256]{1,0:T(8,128)(2,1)} collective-permute-done((bf16[768,256]{1,0:T(8,128)(2,1)S(1)}, bf16[768,256]{1,0:T(8,128)(2,1)}, u32[]{:S(2)}, u32[]{:S(2)}) %collective-permute-start.30) | collective-permute-done | bytes 393248 | tf_op jit(solution)/shard_map/ppermute | solution.py:51
  206.8 13.9 %attn_bwd.1 = (bf16[512,512]{1,0:T(8,128)(2,1)}, bf16[1024,512]{1,0:T(8,128)(2,1)}, bf16[512,512]{1,0:T(8,128)(2,1)}, bf16[512,512]{1,0:T(8,128)(2,1)}, bf16[102...) custom-call(s32[24]{0:T(128)} %pad_add_fusion.3.refs_0_, ...), custom_call_target="tpu_custom_call" | custom-call | flops 2000000000 | tf_op jit(solution)/shard_map/attn_bwd/pallas_call | solution.py:290
  223.1 9.1 %strip_rows.4 = (bf16[256,1536]{1,0:T(8,128)(2,1)}, bf16[256,1536]{1,0:T(8,128)(2,1)}, bf16[256,1536]{1,0:T(8,128)(2,1)}, bf16[256,1536]{1,0:T(8,128)(2,1)}) custom-call(s32[2,4]{1,0:T(2,128)} %pad_add_fusion.1.tbl, bf16[256,2048]{1,0:T(8,128)(2,1)} %copy-done.3, bf16[256,2048]{1,0:T(8,128)(2,1)} %collective-permute-done.18.other_ref.refs_1_, ...), custom_call_target="tpu_custom_call" | custom-call | flops 2400000000 | tf_op jit(solution)/shard_map/strip_rows/pallas_call | solution.py:557
  236.9 5.3 %collective-permute-start.32 = (bf16[1024,512]{1,0:T(8,128)(2,1)}, bf16[1024,512]{1,0:T(8,128)(2,1)S(1)}, u32[]{:S(2)}, u32[]{:S(2)}) collective-permute-start(bf16[1024,512]{1,0:T(8,128)(2,1)} %get-tuple-element.181), channel_id=1, source_target_pairs={{0,4},{4,0},{8,12},{12,8},{16,20},{20,16},{24,28},{28,24},{1,5},{5... | collective-permute-start | bytes 3145736 | tf_op jit(solution)/shard_map/ppermute | solution.py:38
  243.7 16.1 %collective-permute-done.37 = bf16[256,1536]{1,0:T(8,128)(2,1)S(1)} collective-permute-done((bf16[256,1536]{1,0:T(8,128)(2,1)}, bf16[256,1536]{1,0:T(8,128)(2,1)S(1)}, u32[]{:S(2)}, u32[]{:S(2)}) %collective-permute-start.37) | collective-permute-done | bytes 786464 | tf_op jit(solution)/shard_map/ppermute | solution.py:47
  268.7 21.6 %collective-permute-done.64 = bf16[640,256]{1,0:T(8,128)(2,1)S(1)} collective-permute-done((bf16[640,256]{1,0:T(8,128)(2,1)}, bf16[640,256]{1,0:T(8,128)(2,1)S(1)}, u32[]{:S(2)}, u32[]{:S(2)}) %collective-permute-start.64) | collective-permute-done | bytes 327712 | tf_op jit(solution)/shard_map/ppermute | solution.py:51
  301.9 10.9 %collective-permute-done.38.refs_2_ = bf16[1024,512]{1,0:T(8,128)(2,1)} collective-permute-done((bf16[1024,512]{1,0:T(8,128)(2,1)}, bf16[1024,512]{1,0:T(8,128)(2,1)}, u32[]{:S(2)}, u32[]{:S(2)}) %collective-permute-start.38) | collective-permute-done | bytes 1048608 | tf_op jit(solution)/shard_map/ppermute | solution.py:51
  318.9 5.5 %collective-permute-done.45.refs_7_ = bf16[512,640]{1,0:T(8,128)(2,1)} collective-permute-done((bf16[512,640]{1,0:T(8,128)(2,1)}, bf16[512,640]{1,0:T(8,128)(2,1)}, u32[]{:S(2)}, u32[]{:S(2)}) %collective-permute-start.45) | collective-permute-done | bytes 655392 | tf_op jit(solution)/shard_map/ppermute | solution.py:38
  324.4 8.7 %strip_rows.5 = (bf16[256,1280]{1,0:T(8,128)(2,1)}, bf16[256,1280]{1,0:T(8,128)(2,1)}, bf16[256,1280]{1,0:T(8,128)(2,1)}, bf16[256,1280]{1,0:T(8,128)(2,1)}) custom-call(s32[2,4]{1,0:T(2,128)} %pad_add_fusion.1.tbl, bf16[256,2048]{1,0:T(8,128)(2,1)} %copy-done.3, bf16[256,2048]{1,0:T(8,128)(2,1)} %collective-permute-done.18.other_ref.refs_1_, ...), custom_call_target="tpu_custom_call" | custom-call | flops 2100000000 | tf_op jit(solution)/shard_map/strip_rows/pallas_call | solution.py:557
  338.3 18.5 %collective-permute-done.46.refs_4_ = bf16[512,512]{1,0:T(8,128)(2,1)} collective-permute-done((bf16[512,512]{1,0:T(8,128)(2,1)}, bf16[512,512]{1,0:T(8,128)(2,1)}, u32[]{:S(2)}, u32[]{:S(2)}) %collective-permute-start.46) | collective-permute-done | bytes 524320 | tf_op jit(solution)/shard_map/ppermute | solution.py:38
  356.9 5.8 %strip_rows.6 = (bf16[512,512]{1,0:T(8,128)(2,1)}, bf16[256,512]{1,0:T(8,128)(2,1)}, bf16[256,512]{1,0:T(8,128)(2,1)}) custom-call(s32[2,4]{1,0:T(2,128)} %pad_add_fusion.tbl, bf16[512,2048]{1,0:T(8,128)(2,1)} %get-tuple-element.213.x_ref.refs_0_, bf16[256,2048]{1,0:T(8,128)(2,1)} %copy-done, bf16[256,2048]{1,0:T(8,128)(2,1)} %collective-permute-done.21.refs_4_.refs_2_, ...), custom_call_target="tpu_custom_call" | custom-call | flops 1200000000 | tf_op jit(solution)/shard_map/strip_rows/pallas_call | solution.py:557
  371.7 6.1 %project.5 = (bf16[256,2048]{1,0:T(8,128)(2,1)}, bf16[256,2048]{1,0:T(8,128)(2,1)}) custom-call(bf16[512,512]{1,0:T(8,128)(2,1)} %get-tuple-element.202.refs_0_.refs_3_, bf16[2048,512]{1,0:T(8,128)(2,1)} %refs_1_.5, bf16[512,256]{1,0:T(8,128)(2,1)} %get-tuple-element.193.refs_2_.refs_3_, bf16[2048,256]{1,0:T(8,128)(2,1)} %refs_3_.1, ...), custom_call_target="tpu_custom_call" | custom-call | flops 1800000000 | tf_op jit(solution)/shard_map/project/pallas_call | solution.py:349
  391.2 5.8 %strip_rows.7 = (bf16[512,512]{1,0:T(8,128)(2,1)}, bf16[256,512]{1,0:T(8,128)(2,1)}, bf16[256,512]{1,0:T(8,128)(2,1)}) custom-call(s32[2,4]{1,0:T(2,128)} %pad_add_fusion.tbl, bf16[512,2048]{1,0:T(8,128)(2,1)} %get-tuple-element.213.x_ref.refs_0_, bf16[256,2048]{1,0:T(8,128)(2,1)} %copy-done, bf16[256,2048]{1,0:T(8,128)(2,1)} %collective-permute-done.21.refs_4_.refs_2_, ...), custom_call_target="tpu_custom_call" | custom-call | flops 1200000000 | tf_op jit(solution)/shard_map/strip_rows/pallas_call | solution.py:557
  403.2 21.2 %collective-permute-done.62 = bf16[512,512]{1,0:T(8,128)(2,1)} collective-permute-done((bf16[512,512]{1,0:T(8,128)(2,1)}, bf16[512,512]{1,0:T(8,128)(2,1)}, u32[]{:S(2)}, u32[]{:S(2)}) %collective-permute-start.62) | collective-permute-done | bytes 524320 | tf_op jit(solution)/shard_map/ppermute | solution.py:51
  425.5 6.0 %collective-permute-done.52 = bf16[256,512]{1,0:T(8,128)(2,1)S(1)} collective-permute-done((bf16[256,512]{1,0:T(8,128)(2,1)S(1)}, bf16[256,512]{1,0:T(8,128)(2,1)S(1)}, u32[]{:S(2)}, u32[]{:S(2)}) %collective-permute-start.52) | collective-permute-done | bytes 262176 | tf_op jit(solution)/shard_map/ppermute | solution.py:51
  443.4 16.4 %collective-permute-done.59 = bf16[256,1280]{1,0:T(8,128)(2,1)S(1)} collective-permute-done((bf16[256,1280]{1,0:T(8,128)(2,1)S(1)}, bf16[256,1280]{1,0:T(8,128)(2,1)S(1)}, u32[]{:S(2)}, u32[]{:S(2)}) %collective-permute-start.59) | collective-permute-done | bytes 655392 | tf_op jit(solution)/shard_map/ppermute | solution.py:47
  (313 shorter events, 225.9 us)
Async XLA Ops:
  189.0 31.8 %collective-permute-start.34 = (bf16[256,1024]{1,0:T(8,128)(2,1)}, bf16[256,1024]{1,0:T(8,128)(2,1)}, u32[]{:S(2)}, u32[]{:S(2)}) collective-permute-start(bf16[256,1024]{1,0:T(8,128)(2,1)} %pack.4), channel_id=1, source_target_pairs={{0,4},{4,0},{8,12},{12,8},{16,20},{20,16},{24,28},{28,24},{1,5},{5... | collective-permute-start | bytes 1572872 | tf_op jit(solution)/shard_map/ppermute | solution.py:38
  190.2 30.7 %collective-permute-start.33 = (bf16[640,512]{1,0:T(8,128)(2,1)}, bf16[640,512]{1,0:T(8,128)(2,1)}, u32[]{:S(2)}, u32[]{:S(2)}) collective-permute-start(bf16[640,512]{1,0:T(8,128)(2,1)} %get-tuple-element.168), channel_id=1, source_target_pairs={{0,8},{4,12},{8,0},{12,4},{16,24},{20,28},{24,16},{28,20},{1,9},{5... | collective-permute-start | bytes 1966088 | tf_op jit(solution)/shard_map/ppermute | solution.py:51
  191.4 31.2 %collective-permute-start.36 = (bf16[512,768]{1,0:T(8,128)(2,1)}, bf16[512,768]{1,0:T(8,128)(2,1)}, u32[]{:S(2)}, u32[]{:S(2)}) collective-permute-start(bf16[512,768]{1,0:T(8,128)(2,1)} %get-tuple-element.187.up_a.refs_5_), channel_id=1, source_target_pairs={{0,4},{4,0},{8,12},{12,8},{16,20},{20,16},{24,28},{28,24},{1,5},{5... | collective-permute-start | bytes 2359304 | tf_op jit(solution)/shard_map/ppermute | solution.py:38
  232.2 27.6 %collective-permute-start.37 = (bf16[256,1536]{1,0:T(8,128)(2,1)}, bf16[256,1536]{1,0:T(8,128)(2,1)S(1)}, u32[]{:S(2)}, u32[]{:S(2)}) collective-permute-start(bf16[256,1536]{1,0:T(8,128)(2,1)} %get-tuple-element.189), channel_id=1, source_target_pairs={{0,8},{4,12},{8,16},{12,20},{16,24},{20,28},{24,0},{28,4},{1,9},{5... | collective-permute-start | bytes 2359304 | tf_op jit(solution)/shard_map/ppermute | solution.py:47
  236.9 29.6 %collective-permute-start.32 = (bf16[1024,512]{1,0:T(8,128)(2,1)}, bf16[1024,512]{1,0:T(8,128)(2,1)S(1)}, u32[]{:S(2)}, u32[]{:S(2)}) collective-permute-start(bf16[1024,512]{1,0:T(8,128)(2,1)} %get-tuple-element.181), channel_id=1, source_target_pairs={{0,4},{4,0},{8,12},{12,8},{16,20},{20,16},{24,28},{28,24},{1,5},{5... | collective-permute-start | bytes 3145736 | tf_op jit(solution)/shard_map/ppermute | solution.py:38
  242.3 48.0 %collective-permute-start.64 = (bf16[640,256]{1,0:T(8,128)(2,1)}, bf16[640,256]{1,0:T(8,128)(2,1)S(1)}, u32[]{:S(2)}, u32[]{:S(2)}) collective-permute-start(bf16[640,256]{1,0:T(8,128)(2,1)} %add_convert_fusion.13), channel_id=1, source_target_pairs={{0,16},{4,20},{8,24},{12,28},{16,0},{20,4},{24,8},{28,12},{1,17},{... | collective-permute-start | bytes 983048 | tf_op jit(solution)/shard_map/ppermute | solution.py:51
  242.3 55.1 %collective-permute-start.39 = (bf16[512,512]{1,0:T(8,128)(2,1)}, bf16[512,512]{1,0:T(8,128)(2,1)}, u32[]{:S(2)}, u32[]{:S(2)}) collective-permute-start(bf16[512,512]{1,0:T(8,128)(2,1)} %get-tuple-element.192), channel_id=1, source_target_pairs={{0,4},{4,0},{8,12},{12,8},{16,20},{20,16},{24,28},{28,24},{1,5},{5... | collective-permute-start | bytes 1572872 | tf_op jit(solution)/shard_map/ppermute | solution.py:38
  262.1 35.5 %collective-permute-start.55 = (bf16[256,1536]{1,0:T(8,128)(2,1)}, bf16[256,1536]{1,0:T(8,128)(2,1)}, u32[]{:S(2)}, u32[]{:S(2)}) collective-permute-start(bf16[256,1536]{1,0:T(8,128)(2,1)} %add_convert_fusion.7), channel_id=1, source_target_pairs={{0,8},{4,12},{8,16},{12,20},{16,24},{20,28},{24,0},{28,4},{1,9},{5... | collective-permute-start | bytes 2359304 | tf_op jit(solution)/shard_map/ppermute | solution.py:47
  267.8 45.0 %collective-permute-start.38 = (bf16[1024,512]{1,0:T(8,128)(2,1)}, bf16[1024,512]{1,0:T(8,128)(2,1)}, u32[]{:S(2)}, u32[]{:S(2)}) collective-permute-start(bf16[1024,512]{1,0:T(8,128)(2,1)} %add_convert_fusion.1), channel_id=1, source_target_pairs={{0,8},{4,12},{8,0},{12,4},{16,24},{20,28},{24,16},{28,20},{1,9},{5... | collective-permute-start | bytes 3145736 | tf_op jit(solution)/shard_map/ppermute | solution.py:51
  268.3 67.3 %collective-permute-start.28 = (bf16[256,2048]{1,0:T(8,128)(2,1)S(1)}, bf16[256,2048]{1,0:T(8,128)(2,1)}, u32[]{:S(2)}, u32[]{:S(2)}) collective-permute-start(bf16[256,2048]{1,0:T(8,128)(2,1)S(1)} %add_convert_fusion.3), channel_id=1, source_target_pairs={{0,2},{1,3},{2,0},{3,1},{4,6},{5,7},{6,4},{7,5},{8,10},{9,11},{10,... | collective-permute-start | bytes 3145736 | tf_op jit(solution)/shard_map/ppermute | solution.py:34
  290.3 28.6 %collective-permute-start.44 = (bf16[512,640]{1,0:T(8,128)(2,1)}, bf16[512,640]{1,0:T(8,128)(2,1)}, u32[]{:S(2)}, u32[]{:S(2)}) collective-permute-start(bf16[512,640]{1,0:T(8,128)(2,1)} %get-tuple-element.198.gate_b.refs_4_), channel_id=1, source_target_pairs={{0,4},{4,0},{8,12},{12,8},{16,20},{20,16},{24,28},{28,24},{1,5},{5... | collective-permute-start | bytes 1966088 | tf_op jit(solution)/shard_map/ppermute | solution.py:38
  297.5 38.1 %collective-permute-start.48 = (bf16[256,1024]{1,0:T(8,128)(2,1)}, bf16[256,1024]{1,0:T(8,128)(2,1)}, u32[]{:S(2)}, u32[]{:S(2)}) collective-permute-start(bf16[256,1024]{1,0:T(8,128)(2,1)} %get-tuple-element.210), channel_id=1, source_target_pairs={{0,4},{4,0},{8,12},{12,8},{16,20},{20,16},{24,28},{28,24},{1,5},{5... | collective-permute-start | bytes 1572872 | tf_op jit(solution)/shard_map/ppermute | solution.py:38
  312.8 54.2 %collective-permute-start.31 = (bf16[512,512]{1,0:T(8,128)(2,1)}, bf16[512,512]{1,0:T(8,128)(2,1)}, u32[]{:S(2)}, u32[]{:S(2)}) collective-permute-start(bf16[512,512]{1,0:T(8,128)(2,1)} %get-tuple-element.179), channel_id=1, source_target_pairs={{0,4},{4,0},{8,12},{12,8},{16,20},{20,16},{24,28},{28,24},{1,5},{5... | collective-permute-start | bytes 1572872 | tf_op jit(solution)/shard_map/ppermute | solution.py:38
  318.9 38.0 %collective-permute-start.46 = (bf16[512,512]{1,0:T(8,128)(2,1)}, bf16[512,512]{1,0:T(8,128)(2,1)}, u32[]{:S(2)}, u32[]{:S(2)}) collective-permute-start(bf16[512,512]{1,0:T(8,128)(2,1)} %get-tuple-element.202.refs_0_.refs_3_), channel_id=1, source_target_pairs={{0,4},{4,0},{8,12},{12,8},{16,20},{20,16},{24,28},{28,24},{1,5},{5... | collective-permute-start | bytes 1572872 | tf_op jit(solution)/shard_map/ppermute | solution.py:38
  324.4 53.4 %collective-permute-start.56 = (bf16[256,1536]{1,0:T(8,128)(2,1)}, bf16[256,1536]{1,0:T(8,128)(2,1)}, u32[]{:S(2)}, u32[]{:S(2)}) collective-permute-start(bf16[256,1536]{1,0:T(8,128)(2,1)} %add_convert_fusion.6), channel_id=1, source_target_pairs={{0,8},{4,12},{8,16},{12,20},{16,24},{20,28},{24,0},{28,4},{1,9},{5... | collective-permute-start | bytes 2359304 | tf_op jit(solution)/shard_map/ppermute | solution.py:47
  335.6 31.6 %collective-permute-start.40 = (bf16[512,512]{1,0:T(8,128)(2,1)}, bf16[512,512]{1,0:T(8,128)(2,1)}, u32[]{:S(2)}, u32[]{:S(2)}) collective-permute-start(bf16[512,512]{1,0:T(8,128)(2,1)} %add_convert_fusion.10), channel_id=1, source_target_pairs={{0,16},{4,20},{8,24},{12,28},{16,0},{20,4},{24,8},{28,12},{1,17},{... | collective-permute-start | bytes 1572872 | tf_op jit(solution)/shard_map/ppermute | solution.py:51
  367.0 30.8 %collective-permute-start.47 = (bf16[512,512]{1,0:T(8,128)(2,1)}, bf16[512,512]{1,0:T(8,128)(2,1)}, u32[]{:S(2)}, u32[]{:S(2)}) collective-permute-start(bf16[512,512]{1,0:T(8,128)(2,1)} %get-tuple-element.204), channel_id=1, source_target_pairs={{0,8},{4,12},{8,0},{12,4},{16,24},{20,28},{24,16},{28,20},{1,9},{5... | collective-permute-start | bytes 1572872 | tf_op jit(solution)/shard_map/ppermute | solution.py:51
  382.6 41.8 %collective-permute-start.62 = (bf16[512,512]{1,0:T(8,128)(2,1)}, bf16[512,512]{1,0:T(8,128)(2,1)}, u32[]{:S(2)}, u32[]{:S(2)}) collective-permute-start(bf16[512,512]{1,0:T(8,128)(2,1)} %get-tuple-element.212), channel_id=1, source_target_pairs={{0,8},{4,12},{8,0},{12,4},{16,24},{20,28},{24,16},{28,20},{1,9},{5... | collective-permute-start | bytes 1572872 | tf_op jit(solution)/shard_map/ppermute | solution.py:51
  384.6 58.0 %collective-permute-start.41 = (bf16[256,2048]{1,0:T(8,128)(2,1)}, bf16[256,2048]{1,0:T(8,128)(2,1)S(1)}, u32[]{:S(2)}, u32[]{:S(2)}) collective-permute-start(bf16[256,2048]{1,0:T(8,128)(2,1)} %get-tuple-element.196), channel_id=1, source_target_pairs={{0,1},{1,0},{2,3},{3,2},{4,5},{5,4},{6,7},{7,6},{8,9},{9,8},{10,11... | collective-permute-start | bytes 3145736 | tf_op jit(solution)/shard_map/ppermute | solution.py:34
  389.2 47.8 %collective-permute-start.58 = (bf16[256,1280]{1,0:T(8,128)(2,1)}, bf16[256,1280]{1,0:T(8,128)(2,1)}, u32[]{:S(2)}, u32[]{:S(2)}) collective-permute-start(bf16[256,1280]{1,0:T(8,128)(2,1)} %add_convert_fusion.9), channel_id=1, source_target_pairs={{0,8},{4,12},{8,16},{12,20},{16,24},{20,28},{24,0},{28,4},{1,9},{5... | collective-permute-start | bytes 1966088 | tf_op jit(solution)/shard_map/ppermute | solution.py:47
  397.1 42.4 %collective-permute-start.53 = (bf16[512,512]{1,0:T(8,128)(2,1)}, bf16[512,512]{1,0:T(8,128)(2,1)S(1)}, u32[]{:S(2)}, u32[]{:S(2)}) collective-permute-start(bf16[512,512]{1,0:T(8,128)(2,1)} %get-tuple-element.214), channel_id=1, source_target_pairs={{0,8},{4,12},{8,0},{12,4},{16,24},{20,28},{24,16},{28,20},{1,9},{5... | collective-permute-start | bytes 1572872 | tf_op jit(solution)/shard_map/ppermute | solution.py:51
  398.9 32.6 %collective-permute-start.52 = (bf16[256,512]{1,0:T(8,128)(2,1)S(1)}, bf16[256,512]{1,0:T(8,128)(2,1)S(1)}, u32[]{:S(2)}, u32[]{:S(2)}) collective-permute-start(bf16[256,512]{1,0:T(8,128)(2,1)S(1)} %add_convert_fusion.16), channel_id=1, source_target_pairs={{0,16},{4,20},{8,24},{12,28},{16,0},{20,4},{24,8},{28,12},{1,17},{... | collective-permute-start | bytes 786440 | tf_op jit(solution)/shard_map/ppermute | solution.py:51
  431.5 44.0 %collective-permute-start.63 = (bf16[512,256]{1,0:T(8,128)(2,1)S(1)}, bf16[512,256]{1,0:T(8,128)(2,1)S(1)}, u32[]{:S(2)}, u32[]{:S(2)}) collective-permute-start(bf16[512,256]{1,0:T(8,128)(2,1)S(1)} %add_convert_fusion.14), channel_id=1, source_target_pairs={{0,16},{4,20},{8,24},{12,28},{16,0},{20,4},{24,8},{28,12},{1,17},{... | collective-permute-start | bytes 786440 | tf_op jit(solution)/shard_map/ppermute | solution.py:51
  439.6 32.6 %collective-permute-start.54 = (bf16[256,512]{1,0:T(8,128)(2,1)S(1)}, bf16[256,512]{1,0:T(8,128)(2,1)S(1)}, u32[]{:S(2)}, u32[]{:S(2)}) collective-permute-start(bf16[256,512]{1,0:T(8,128)(2,1)S(1)} %add_convert_fusion.15), channel_id=1, source_target_pairs={{0,16},{4,20},{8,24},{12,28},{16,0},{20,4},{24,8},{28,12},{1,17},{... | collective-permute-start | bytes 786440 | tf_op jit(solution)/shard_map/ppermute | solution.py:51
  (93 other events, 1251.5 us)

commit v3 on v2

--- a/solution.py
+++ b/solution.py
@@ -912,10 +912,10 @@
     pairs = [
         (n.astype(F32) + f.astype(F32)).astype(BF) for n, f in zip(d_near[:-1], d_far[:-1])
     ]
-    kv_got, kv_mid = halve([*pairs, d_near[-1]], 0)
+    dgu_b_near = [wide_swap(after(v, d_query)) for v in dgu_b]
+    kv_got, kv_mid = halve([*pairs, d_near[-1]], 0, dgu_b_near[0])
     d_key, d_value = close_kv([d_near[-1], d_far[-1], *kv_got], cosine, sine)
 
-    dgu_b_near = [wide_swap(after(v, d_query)) for v in dgu_b]
     gate_up_b = strip_rows_grad(
         [after(normed_two, gate_up_a_mid, kv_mid), normed_two_other],
         normed_two_sides,

time: 491 us -> 488 us (level)
  starting transfers between devices: 72.1 us -> 65.6 us
    ppermute x23, starting transfers between devices: 39.1 us -> 21.5 us  [wide_swap(): lax.ppermute(value, 'wide', [(w, w ^ 1) for w in range(lax.axis_size('wid...]
    ppermute x12, starting transfers between devices: 10.7 us -> 24.1 us  [wide_flip(): lax.ppermute(value, 'wide', [(w, w ^ 2 << bit) for w in range(lax.axis_si...]
    ppermute x23, waiting for transfers between devices: 43 us -> 37.1 us  [wide_swap(): lax.ppermute(value, 'wide', [(w, w ^ 1) for w in range(lax.axis_size('wid...]
    ppermute x12, waiting for transfers between devices: 74.3 us -> 80 us  [wide_flip(): lax.ppermute(value, 'wide', [(w, w ^ 2 << bit) for w in range(lax.axis_si...]
  transfers between devices with their start and end apart: 65 -> 65, of which waited for: 30 -> 31; matrix products, arithmetic and copies ran while one was open for 12% -> 12% of each run, Pallas kernels for 26% -> 27%
where the time goes in v3:
time: 488 us; the launch traced here: 481 us
  waiting for transfers between devices  194 us (40%)
  Pallas kernels  150 us (31%)
  starting transfers between devices  65.6 us (13%)
  other arithmetic  62.4 us (13%)
  local copies, waits for them, and re-layouts  7.45 us (2%)
    ppermute x12, waiting for transfers between devices, wide_flip(): lax.ppermute(value, 'wide', [(w, w ^ 2 << bit) for w in range(lax.axis_si...  80 us
    ppermute x13, waiting for transfers between devices, wide_ring(): return lax.ppermute(value, 'wide', pairs)  44.7 us
    ppermute x23, waiting for transfers between devices, wide_swap(): lax.ppermute(value, 'wide', [(w, w ^ 1) for w in range(lax.axis_size('wid...  37.1 us
    ppermute x17, waiting for transfers between devices, narrow_swap(): return lax.ppermute(value, 'narrow', pairs)  32.2 us
    pallas_call x4, Pallas kernels, strip_rows_grad(): pl.pallas_call(functools.partial(strip_rows_kernel, len(left), len(left_n...  29.6 us
    ppermute x12, starting transfers between devices, wide_flip(): lax.ppermute(value, 'wide', [(w, w ^ 2 << bit) for w in range(lax.axis_si...  24.1 us
    ppermute x23, starting transfers between devices, wide_swap(): lax.ppermute(value, 'wide', [(w, w ^ 1) for w in range(lax.axis_size('wid...  21.5 us
    pallas_call x3, Pallas kernels, project(): pl.pallas_call(functools.partial(project_kernel, plan), out_shape=[jax.Sh...  16.8 us
  transfers between devices with their start and end apart: 65, of which 31 were waited for; matrix products, arithmetic and copies ran while one was open for 12% of the time, Pallas kernels for 27%

profile of v3, /device:TPU:0, one launch (start us, length us, event | category | flops | bytes accessed | tf_op | source)
XLA Modules:
  0.0 481.2 jit_solution(16315618625202844853)
XLA Ops:
  29.6 8.6 %inner_grad.1.di_ref = f32[512,1408]{1,0:T(8,128)} custom-call(bf16[512,2048]{1,0:T(8,128)(2,1)} %maximum_select_fusion.x_ref.refs_1_, bf16[1408,2048]{1,0:T(8,128)(2,1)} %refs_1_.4), custom_call_target="tpu_custom_call" | custom-call | flops 2400000000 | tf_op jit(solution)/shard_map/inner_grad/pallas_call | solution.py:450
  60.4 6.4 %attn_fwd.2 = (bf16[512,512]{1,0:T(8,128)(2,1)}, f32[2,512]{1,0:T(2,128)}) custom-call(s32[24]{0:T(128)} %pad_add_fusion.3.refs_0_, bf16[512,512]{1,0:T(8,128)(2,1)} %query_proj.1.refs_1_, s32[1,512]{1,0:T(1,128)} %bitcast.32, s32[1,512]{1,0:T(1,128)} %bitcast.29, bf16[512,256]{1,0:T(8,128)(2,1)} %get-tuple-element.125.refs_4_.refs_10_, ...), custom_call_target="tpu_custom_call" | custom-call | flops 1000000000 | tf_op jit(solution)/shard_map/attn_fwd/pallas_call | solution.py:200
  66.9 6.6 %attn_fwd.3 = (bf16[512,512]{1,0:T(8,128)(2,1)}, f32[2,512]{1,0:T(2,128)}) custom-call(s32[24]{0:T(128)} %pad_add_fusion.3.refs_0_, bf16[512,512]{1,0:T(8,128)(2,1)} %query_proj.1.refs_1_, s32[1,512]{1,0:T(1,128)} %bitcast.33, s32[1,512]{1,0:T(1,128)} %bitcast.30, ...), custom_call_target="tpu_custom_call", output_to_operand_aliasing={{0}: (12, {})} | custom-call | flops 1000000000 | tf_op jit(solution)/shard_map/attn_fwd/pallas_call | solution.py:200
  88.4 22.7 %collective-permute-done.16 = bf16[256,2048]{1,0:T(8,128)(2,1)S(1)} collective-permute-done((bf16[256,2048]{1,0:T(8,128)(2,1)S(1)}, bf16[256,2048]{1,0:T(8,128)(2,1)S(1)}, u32[]{:S(2)}, u32[]{:S(2)}) %collective-permute-start.16) | collective-permute-done | bytes 1048608 | tf_op jit(solution)/shard_map/ppermute | solution.py:34
  116.3 8.2 %gated.2 = (bf16[512,768]{1,0:T(8,128)(2,1)}, bf16[512,768]{1,0:T(8,128)(2,1)}, bf16[512,768]{1,0:T(8,128)(2,1)}) custom-call(bf16[256,2048]{1,0:T(8,128)(2,1)} %copy-done.3, bf16[256,2048]{1,0:T(8,128)(2,1)} %collective-permute-done.18.other_ref.refs_1_, bf16[2048,1408]{1,0:T(8,128)(2,1)} %wg_ref.5, bf16[2048,1408]{1,0:T(8,128)(2,1)} %wu_ref.5, ...), custom_call_target="tpu_custom_call" | custom-call | flops 2249999872 | tf_op jit(solution)/shard_map/gated/pallas_call | solution.py:409
  125.5 7.7 %gated.3 = (bf16[512,640]{1,0:T(8,128)(2,1)}, bf16[512,640]{1,0:T(8,128)(2,1)}, bf16[512,640]{1,0:T(8,128)(2,1)}) custom-call(bf16[256,2048]{1,0:T(8,128)(2,1)} %copy-done.3, bf16[256,2048]{1,0:T(8,128)(2,1)} %collective-permute-done.18.other_ref.refs_1_, bf16[2048,1408]{1,0:T(8,128)(2,1)} %wg_ref.5, bf16[2048,1408]{1,0:T(8,128)(2,1)} %wu_ref.5, ...), custom_call_target="tpu_custom_call" | custom-call | flops 2249999872 | tf_op jit(solution)/shard_map/gated/pallas_call | solution.py:409
  133.2 10.8 %back_dense.1 = (bf16[256,2048]{1,0:T(8,128)(2,1)}, bf16[256,2048]{1,0:T(8,128)(2,1)}) custom-call(bf16[512,768]{1,0:T(8,128)(2,1)} %get-tuple-element.172.gate_a.refs_4_, bf16[512,768]{1,0:T(8,128)(2,1)} %get-tuple-element.189.up_a.refs_5_, bf16[512,640]{1,0:T(8,128)(2,1)} %get-tuple-element.193.gate_b.refs_4_, ...), custom_call_target="tpu_custom_call" | custom-call | flops 3300000000 | tf_op jit(solution)/shard_map/back_dense/pallas_call | solution.py:377
  157.5 5.4 %collective-permute-done.22.refs_1_ = bf16[512,640]{1,0:T(8,128)(2,1)} collective-permute-done((bf16[512,640]{1,0:T(8,128)(2,1)}, bf16[512,640]{1,0:T(8,128)(2,1)}, u32[]{:S(2)}, u32[]{:S(2)}) %collective-permute-start.22) | collective-permute-done | bytes 655392 | tf_op jit(solution)/shard_map/ppermute | solution.py:38
  162.9 7.1 %project.4 = (bf16[256,2048]{1,0:T(8,128)(2,1)}, bf16[256,2048]{1,0:T(8,128)(2,1)}) custom-call(bf16[512,768]{1,0:T(8,128)(2,1)} %get-tuple-element.166.refs_0_, bf16[1408,2048]{1,0:T(8,128)(2,1)} %refs_1_.4, bf16[512,640]{1,0:T(8,128)(2,1)} %get-tuple-element.169.refs_2_.refs_0_), custom_call_target="tpu_custom_call" | custom-call | flops 1800000000 | tf_op jit(solution)/shard_map/project/pallas_call | solution.py:349
  197.2 7.6 %collective-permute-done.30 = bf16[768,256]{1,0:T(8,128)(2,1)} collective-permute-done((bf16[768,256]{1,0:T(8,128)(2,1)S(1)}, bf16[768,256]{1,0:T(8,128)(2,1)}, u32[]{:S(2)}, u32[]{:S(2)}) %collective-permute-start.30) | collective-permute-done | bytes 393248 | tf_op jit(solution)/shard_map/ppermute | solution.py:51
  204.8 15.3 %attn_bwd.1 = (bf16[512,512]{1,0:T(8,128)(2,1)}, bf16[1024,512]{1,0:T(8,128)(2,1)}, bf16[512,512]{1,0:T(8,128)(2,1)}, bf16[512,512]{1,0:T(8,128)(2,1)}, bf16[102...) custom-call(s32[24]{0:T(128)} %pad_add_fusion.3.refs_0_, ...), custom_call_target="tpu_custom_call" | custom-call | flops 2000000000 | tf_op jit(solution)/shard_map/attn_bwd/pallas_call | solution.py:290
  222.5 9.2 %strip_rows.4 = (bf16[256,1536]{1,0:T(8,128)(2,1)}, bf16[256,1536]{1,0:T(8,128)(2,1)}, bf16[256,1536]{1,0:T(8,128)(2,1)}, bf16[256,1536]{1,0:T(8,128)(2,1)}) custom-call(s32[2,4]{1,0:T(2,128)} %pad_add_fusion.1.tbl, bf16[256,2048]{1,0:T(8,128)(2,1)} %copy-done.3, bf16[256,2048]{1,0:T(8,128)(2,1)} %collective-permute-done.18.other_ref.refs_1_, ...), custom_call_target="tpu_custom_call" | custom-call | flops 2400000000 | tf_op jit(solution)/shard_map/strip_rows/pallas_call | solution.py:557
  234.0 8.0 %collective-permute-start.64 = (bf16[640,256]{1,0:T(8,128)(2,1)}, bf16[640,256]{1,0:T(8,128)(2,1)S(1)}, u32[]{:S(2)}, u32[]{:S(2)}) collective-permute-start(bf16[640,256]{1,0:T(8,128)(2,1)} %add_convert_fusion.13), channel_id=1, source_target_pairs={{0,16},{4,20},{8,24},{12,28},{16,0},{20,4},{24,8},{28,12},{1,17},{... | collective-permute-start | bytes 983048 | tf_op jit(solution)/shard_map/ppermute | solution.py:51
  244.0 16.1 %collective-permute-done.37 = bf16[256,1536]{1,0:T(8,128)(2,1)S(1)} collective-permute-done((bf16[256,1536]{1,0:T(8,128)(2,1)}, bf16[256,1536]{1,0:T(8,128)(2,1)S(1)}, u32[]{:S(2)}, u32[]{:S(2)}) %collective-permute-start.37) | collective-permute-done | bytes 786464 | tf_op jit(solution)/shard_map/ppermute | solution.py:47
  267.5 23.1 %collective-permute-done.64 = bf16[640,256]{1,0:T(8,128)(2,1)S(1)} collective-permute-done((bf16[640,256]{1,0:T(8,128)(2,1)}, bf16[640,256]{1,0:T(8,128)(2,1)S(1)}, u32[]{:S(2)}, u32[]{:S(2)}) %collective-permute-start.64) | collective-permute-done | bytes 327712 | tf_op jit(solution)/shard_map/ppermute | solution.py:51
  298.1 13.9 %collective-permute-done.38.refs_2_ = bf16[1024,512]{1,0:T(8,128)(2,1)} collective-permute-done((bf16[1024,512]{1,0:T(8,128)(2,1)}, bf16[1024,512]{1,0:T(8,128)(2,1)}, u32[]{:S(2)}, u32[]{:S(2)}) %collective-permute-start.38) | collective-permute-done | bytes 1048608 | tf_op jit(solution)/shard_map/ppermute | solution.py:51
  319.7 8.8 %strip_rows.5 = (bf16[256,1280]{1,0:T(8,128)(2,1)}, bf16[256,1280]{1,0:T(8,128)(2,1)}, bf16[256,1280]{1,0:T(8,128)(2,1)}, bf16[256,1280]{1,0:T(8,128)(2,1)}) custom-call(s32[2,4]{1,0:T(2,128)} %pad_add_fusion.1.tbl, bf16[256,2048]{1,0:T(8,128)(2,1)} %copy-done.3, bf16[256,2048]{1,0:T(8,128)(2,1)} %collective-permute-done.18.other_ref.refs_1_, ...), custom_call_target="tpu_custom_call" | custom-call | flops 2100000000 | tf_op jit(solution)/shard_map/strip_rows/pallas_call | solution.py:557
  333.7 18.8 %collective-permute-done.46.refs_4_ = bf16[512,512]{1,0:T(8,128)(2,1)} collective-permute-done((bf16[512,512]{1,0:T(8,128)(2,1)}, bf16[512,512]{1,0:T(8,128)(2,1)}, u32[]{:S(2)}, u32[]{:S(2)}) %collective-permute-start.46) | collective-permute-done | bytes 524320 | tf_op jit(solution)/shard_map/ppermute | solution.py:38
  352.5 5.8 %strip_rows.6 = (bf16[512,512]{1,0:T(8,128)(2,1)}, bf16[256,512]{1,0:T(8,128)(2,1)}, bf16[256,512]{1,0:T(8,128)(2,1)}) custom-call(s32[2,4]{1,0:T(2,128)} %pad_add_fusion.tbl, bf16[512,2048]{1,0:T(8,128)(2,1)} %get-tuple-element.217.x_ref.refs_0_, bf16[256,2048]{1,0:T(8,128)(2,1)} %copy-done, bf16[256,2048]{1,0:T(8,128)(2,1)} %collective-permute-done.21.refs_4_.refs_2_, ...), custom_call_target="tpu_custom_call" | custom-call | flops 1200000000 | tf_op jit(solution)/shard_map/strip_rows/pallas_call | solution.py:557
  369.7 6.1 %project.5 = (bf16[256,2048]{1,0:T(8,128)(2,1)}, bf16[256,2048]{1,0:T(8,128)(2,1)}) custom-call(bf16[512,512]{1,0:T(8,128)(2,1)} %get-tuple-element.206.refs_0_.refs_3_, bf16[2048,512]{1,0:T(8,128)(2,1)} %refs_1_.5, bf16[512,256]{1,0:T(8,128)(2,1)} %get-tuple-element.198.refs_2_.refs_3_, bf16[2048,256]{1,0:T(8,128)(2,1)} %refs_3_.1, ...), custom_call_target="tpu_custom_call" | custom-call | flops 1800000000 | tf_op jit(solution)/shard_map/project/pallas_call | solution.py:349
  390.5 5.8 %strip_rows.7 = (bf16[512,512]{1,0:T(8,128)(2,1)}, bf16[256,512]{1,0:T(8,128)(2,1)}, bf16[256,512]{1,0:T(8,128)(2,1)}) custom-call(s32[2,4]{1,0:T(2,128)} %pad_add_fusion.tbl, bf16[512,2048]{1,0:T(8,128)(2,1)} %get-tuple-element.217.x_ref.refs_0_, bf16[256,2048]{1,0:T(8,128)(2,1)} %copy-done, bf16[256,2048]{1,0:T(8,128)(2,1)} %collective-permute-done.21.refs_4_.refs_2_, ...), custom_call_target="tpu_custom_call" | custom-call | flops 1200000000 | tf_op jit(solution)/shard_map/strip_rows/pallas_call | solution.py:557
  402.4 19.9 %collective-permute-done.62 = bf16[512,512]{1,0:T(8,128)(2,1)} collective-permute-done((bf16[512,512]{1,0:T(8,128)(2,1)}, bf16[512,512]{1,0:T(8,128)(2,1)}, u32[]{:S(2)}, u32[]{:S(2)}) %collective-permute-start.62) | collective-permute-done | bytes 524320 | tf_op jit(solution)/shard_map/ppermute | solution.py:51
  423.4 6.8 %collective-permute-done.52 = bf16[256,512]{1,0:T(8,128)(2,1)S(1)} collective-permute-done((bf16[256,512]{1,0:T(8,128)(2,1)S(1)}, bf16[256,512]{1,0:T(8,128)(2,1)S(1)}, u32[]{:S(2)}, u32[]{:S(2)}) %collective-permute-start.52) | collective-permute-done | bytes 262176 | tf_op jit(solution)/shard_map/ppermute | solution.py:51
  442.3 16.2 %collective-permute-done.59 = bf16[256,1280]{1,0:T(8,128)(2,1)S(1)} collective-permute-done((bf16[256,1280]{1,0:T(8,128)(2,1)S(1)}, bf16[256,1280]{1,0:T(8,128)(2,1)S(1)}, u32[]{:S(2)}, u32[]{:S(2)}) %collective-permute-start.59) | collective-permute-done | bytes 655392 | tf_op jit(solution)/shard_map/ppermute | solution.py:47
  (313 shorter events, 214.5 us)
Async XLA Ops:
  189.1 31.1 %collective-permute-start.34 = (bf16[256,1024]{1,0:T(8,128)(2,1)}, bf16[256,1024]{1,0:T(8,128)(2,1)}, u32[]{:S(2)}, u32[]{:S(2)}) collective-permute-start(bf16[256,1024]{1,0:T(8,128)(2,1)} %pack.4), channel_id=1, source_target_pairs={{0,4},{4,0},{8,12},{12,8},{16,20},{20,16},{24,28},{28,24},{1,5},{5... | collective-permute-start | bytes 1572872 | tf_op jit(solution)/shard_map/ppermute | solution.py:38
  190.1 30.1 %collective-permute-start.33 = (bf16[640,512]{1,0:T(8,128)(2,1)}, bf16[640,512]{1,0:T(8,128)(2,1)}, u32[]{:S(2)}, u32[]{:S(2)}) collective-permute-start(bf16[640,512]{1,0:T(8,128)(2,1)} %get-tuple-element.170), channel_id=1, source_target_pairs={{0,8},{4,12},{8,0},{12,4},{16,24},{20,28},{24,16},{28,20},{1,9},{5... | collective-permute-start | bytes 1966088 | tf_op jit(solution)/shard_map/ppermute | solution.py:51
  191.8 30.2 %collective-permute-start.36 = (bf16[512,768]{1,0:T(8,128)(2,1)}, bf16[512,768]{1,0:T(8,128)(2,1)}, u32[]{:S(2)}, u32[]{:S(2)}) collective-permute-start(bf16[512,768]{1,0:T(8,128)(2,1)} %get-tuple-element.189.up_a.refs_5_), channel_id=1, source_target_pairs={{0,4},{4,0},{8,12},{12,8},{16,20},{20,16},{24,28},{28,24},{1,5},{5... | collective-permute-start | bytes 2359304 | tf_op jit(solution)/shard_map/ppermute | solution.py:38
  234.0 32.5 %collective-permute-start.27 = (bf16[256,2048]{1,0:T(8,128)(2,1)S(1)}, bf16[256,2048]{1,0:T(8,128)(2,1)S(1)}, u32[]{:S(2)}, u32[]{:S(2)}) collective-permute-start(bf16[256,2048]{1,0:T(8,128)(2,1)S(1)} %copy-done.35), channel_id=1, source_target_pairs={{0,1},{1,0},{2,3},{3,2},{4,5},{5,4},{6,7},{7,6},{8,9},{9,8},{10,11... | collective-permute-start | bytes 3145736 | tf_op jit(solution)/shard_map/ppermute | solution.py:34
  234.0 56.6 %collective-permute-start.64 = (bf16[640,256]{1,0:T(8,128)(2,1)}, bf16[640,256]{1,0:T(8,128)(2,1)S(1)}, u32[]{:S(2)}, u32[]{:S(2)}) collective-permute-start(bf16[640,256]{1,0:T(8,128)(2,1)} %add_convert_fusion.13), channel_id=1, source_target_pairs={{0,16},{4,20},{8,24},{12,28},{16,0},{20,4},{24,8},{28,12},{1,17},{... | collective-permute-start | bytes 983048 | tf_op jit(solution)/shard_map/ppermute | solution.py:51
  242.0 51.6 %collective-permute-start.39 = (bf16[512,640]{1,0:T(8,128)(2,1)}, bf16[512,640]{1,0:T(8,128)(2,1)}, u32[]{:S(2)}, u32[]{:S(2)}) collective-permute-start(bf16[512,640]{1,0:T(8,128)(2,1)} %get-tuple-element.193.gate_b.refs_4_), channel_id=1, source_target_pairs={{0,4},{4,0},{8,12},{12,8},{16,20},{20,16},{24,28},{28,24},{1,5},{5... | collective-permute-start | bytes 1966088 | tf_op jit(solution)/shard_map/ppermute | solution.py:38
  262.3 33.2 %collective-permute-start.55 = (bf16[256,1536]{1,0:T(8,128)(2,1)}, bf16[256,1536]{1,0:T(8,128)(2,1)}, u32[]{:S(2)}, u32[]{:S(2)}) collective-permute-start(bf16[256,1536]{1,0:T(8,128)(2,1)} %add_convert_fusion.7), channel_id=1, source_target_pairs={{0,8},{4,12},{8,16},{12,20},{16,24},{20,28},{24,0},{28,4},{1,9},{5... | collective-permute-start | bytes 2359304 | tf_op jit(solution)/shard_map/ppermute | solution.py:47
  264.1 47.9 %collective-permute-start.38 = (bf16[1024,512]{1,0:T(8,128)(2,1)}, bf16[1024,512]{1,0:T(8,128)(2,1)}, u32[]{:S(2)}, u32[]{:S(2)}) collective-permute-start(bf16[1024,512]{1,0:T(8,128)(2,1)} %add_convert_fusion.1), channel_id=1, source_target_pairs={{0,8},{4,12},{8,0},{12,4},{16,24},{20,28},{24,16},{28,20},{1,9},{5... | collective-permute-start | bytes 3145736 | tf_op jit(solution)/shard_map/ppermute | solution.py:51
  266.9 64.0 %collective-permute-start.28 = (bf16[256,2048]{1,0:T(8,128)(2,1)S(1)}, bf16[256,2048]{1,0:T(8,128)(2,1)}, u32[]{:S(2)}, u32[]{:S(2)}) collective-permute-start(bf16[256,2048]{1,0:T(8,128)(2,1)S(1)} %add_convert_fusion.3), channel_id=1, source_target_pairs={{0,2},{1,3},{2,0},{3,1},{4,6},{5,7},{6,4},{7,5},{8,10},{9,11},{10,... | collective-permute-start | bytes 3145736 | tf_op jit(solution)/shard_map/ppermute | solution.py:34
  295.5 35.4 %collective-permute-start.48 = (bf16[256,1024]{1,0:T(8,128)(2,1)}, bf16[256,1024]{1,0:T(8,128)(2,1)}, u32[]{:S(2)}, u32[]{:S(2)}) collective-permute-start(bf16[256,1024]{1,0:T(8,128)(2,1)} %get-tuple-element.214), channel_id=1, source_target_pairs={{0,4},{4,0},{8,12},{12,8},{16,20},{20,16},{24,28},{28,24},{1,5},{5... | collective-permute-start | bytes 1572872 | tf_op jit(solution)/shard_map/ppermute | solution.py:38
  312.0 54.4 %collective-permute-start.31 = (bf16[512,512]{1,0:T(8,128)(2,1)}, bf16[512,512]{1,0:T(8,128)(2,1)}, u32[]{:S(2)}, u32[]{:S(2)}) collective-permute-start(bf16[512,512]{1,0:T(8,128)(2,1)} %get-tuple-element.181), channel_id=1, source_target_pairs={{0,4},{4,0},{8,12},{12,8},{16,20},{20,16},{24,28},{28,24},{1,5},{5... | collective-permute-start | bytes 1572872 | tf_op jit(solution)/shard_map/ppermute | solution.py:38
  312.8 39.7 %collective-permute-start.46 = (bf16[512,512]{1,0:T(8,128)(2,1)}, bf16[512,512]{1,0:T(8,128)(2,1)}, u32[]{:S(2)}, u32[]{:S(2)}) collective-permute-start(bf16[512,512]{1,0:T(8,128)(2,1)} %get-tuple-element.206.refs_0_.refs_3_), channel_id=1, source_target_pairs={{0,4},{4,0},{8,12},{12,8},{16,20},{20,16},{24,28},{28,24},{1,5},{5... | collective-permute-start | bytes 1572872 | tf_op jit(solution)/shard_map/ppermute | solution.py:38
  319.7 56.0 %collective-permute-start.56 = (bf16[256,1536]{1,0:T(8,128)(2,1)}, bf16[256,1536]{1,0:T(8,128)(2,1)}, u32[]{:S(2)}, u32[]{:S(2)}) collective-permute-start(bf16[256,1536]{1,0:T(8,128)(2,1)} %add_convert_fusion.6), channel_id=1, source_target_pairs={{0,8},{4,12},{8,16},{12,20},{16,24},{20,28},{24,0},{28,4},{1,9},{5... | collective-permute-start | bytes 2359304 | tf_op jit(solution)/shard_map/ppermute | solution.py:47
  331.0 31.0 %collective-permute-start.41 = (bf16[512,512]{1,0:T(8,128)(2,1)}, bf16[512,512]{1,0:T(8,128)(2,1)}, u32[]{:S(2)}, u32[]{:S(2)}) collective-permute-start(bf16[512,512]{1,0:T(8,128)(2,1)} %add_convert_fusion.10), channel_id=1, source_target_pairs={{0,16},{4,20},{8,24},{12,28},{16,0},{20,4},{24,8},{28,12},{1,17},{... | collective-permute-start | bytes 1572872 | tf_op jit(solution)/shard_map/ppermute | solution.py:51
  331.0 31.3 %collective-permute-start.49 = (bf16[256,1024]{1,0:T(8,128)(2,1)}, bf16[256,1024]{1,0:T(8,128)(2,1)}, u32[]{:S(2)}, u32[]{:S(2)}) collective-permute-start(bf16[256,1024]{1,0:T(8,128)(2,1)} %collective-permute-done.48.refs_4_), channel_id=1, source_target_pairs={{0,1},{1,0},{2,3},{3,2},{4,5},{5,4},{6,7},{7,6},{8,9},{9,8},{10,11... | collective-permute-start | bytes 1572872 | tf_op jit(solution)/shard_map/ppermute | solution.py:34
  352.5 30.4 %collective-permute-start.29 = (bf16[256,2048]{1,0:T(8,128)(2,1)}, bf16[256,2048]{1,0:T(8,128)(2,1)S(1)}, u32[]{:S(2)}, u32[]{:S(2)}) collective-permute-start(bf16[256,2048]{1,0:T(8,128)(2,1)} %add_convert_fusion.2), channel_id=1, source_target_pairs={{0,1},{1,0},{2,3},{3,2},{4,5},{5,4},{6,7},{7,6},{8,9},{9,8},{10,11... | collective-permute-start | bytes 3145736 | tf_op jit(solution)/shard_map/ppermute | solution.py:34
  362.3 34.8 %collective-permute-start.47 = (bf16[512,512]{1,0:T(8,128)(2,1)}, bf16[512,512]{1,0:T(8,128)(2,1)}, u32[]{:S(2)}, u32[]{:S(2)}) collective-permute-start(bf16[512,512]{1,0:T(8,128)(2,1)} %get-tuple-element.208), channel_id=1, source_target_pairs={{0,8},{4,12},{8,0},{12,4},{16,24},{20,28},{24,16},{28,20},{1,9},{5... | collective-permute-start | bytes 1572872 | tf_op jit(solution)/shard_map/ppermute | solution.py:51
  381.8 40.5 %collective-permute-start.62 = (bf16[512,512]{1,0:T(8,128)(2,1)}, bf16[512,512]{1,0:T(8,128)(2,1)}, u32[]{:S(2)}, u32[]{:S(2)}) collective-permute-start(bf16[512,512]{1,0:T(8,128)(2,1)} %get-tuple-element.216), channel_id=1, source_target_pairs={{0,8},{4,12},{8,0},{12,4},{16,24},{20,28},{24,16},{28,20},{1,9},{5... | collective-permute-start | bytes 1572872 | tf_op jit(solution)/shard_map/ppermute | solution.py:51
  383.9 57.4 %collective-permute-start.42 = (bf16[256,2048]{1,0:T(8,128)(2,1)}, bf16[256,2048]{1,0:T(8,128)(2,1)S(1)}, u32[]{:S(2)}, u32[]{:S(2)}) collective-permute-start(bf16[256,2048]{1,0:T(8,128)(2,1)} %get-tuple-element.201), channel_id=1, source_target_pairs={{0,1},{1,0},{2,3},{3,2},{4,5},{5,4},{6,7},{7,6},{8,9},{9,8},{10,11... | collective-permute-start | bytes 3145736 | tf_op jit(solution)/shard_map/ppermute | solution.py:34
  388.5 47.2 %collective-permute-start.58 = (bf16[256,1280]{1,0:T(8,128)(2,1)}, bf16[256,1280]{1,0:T(8,128)(2,1)}, u32[]{:S(2)}, u32[]{:S(2)}) collective-permute-start(bf16[256,1280]{1,0:T(8,128)(2,1)} %add_convert_fusion.9), channel_id=1, source_target_pairs={{0,8},{4,12},{8,16},{12,20},{16,24},{20,28},{24,0},{28,4},{1,9},{5... | collective-permute-start | bytes 1966088 | tf_op jit(solution)/shard_map/ppermute | solution.py:47
  396.3 41.9 %collective-permute-start.53 = (bf16[512,512]{1,0:T(8,128)(2,1)}, bf16[512,512]{1,0:T(8,128)(2,1)S(1)}, u32[]{:S(2)}, u32[]{:S(2)}) collective-permute-start(bf16[512,512]{1,0:T(8,128)(2,1)} %get-tuple-element.218), channel_id=1, source_target_pairs={{0,8},{4,12},{8,0},{12,4},{16,24},{20,28},{24,16},{28,20},{1,9},{5... | collective-permute-start | bytes 1572872 | tf_op jit(solution)/shard_map/ppermute | solution.py:51
  398.2 32.1 %collective-permute-start.52 = (bf16[256,512]{1,0:T(8,128)(2,1)S(1)}, bf16[256,512]{1,0:T(8,128)(2,1)S(1)}, u32[]{:S(2)}, u32[]{:S(2)}) collective-permute-start(bf16[256,512]{1,0:T(8,128)(2,1)S(1)} %add_convert_fusion.16), channel_id=1, source_target_pairs={{0,16},{4,20},{8,24},{12,28},{16,0},{20,4},{24,8},{28,12},{1,17},{... | collective-permute-start | bytes 786440 | tf_op jit(solution)/shard_map/ppermute | solution.py:51
  430.3 43.8 %collective-permute-start.63 = (bf16[512,256]{1,0:T(8,128)(2,1)S(1)}, bf16[512,256]{1,0:T(8,128)(2,1)S(1)}, u32[]{:S(2)}, u32[]{:S(2)}) collective-permute-start(bf16[512,256]{1,0:T(8,128)(2,1)S(1)} %add_convert_fusion.14), channel_id=1, source_target_pairs={{0,16},{4,20},{8,24},{12,28},{16,0},{20,4},{24,8},{28,12},{1,17},{... | collective-permute-start | bytes 786440 | tf_op jit(solution)/shard_map/ppermute | solution.py:51
  438.3 32.5 %collective-permute-start.54 = (bf16[256,512]{1,0:T(8,128)(2,1)S(1)}, bf16[256,512]{1,0:T(8,128)(2,1)S(1)}, u32[]{:S(2)}, u32[]{:S(2)}) collective-permute-start(bf16[256,512]{1,0:T(8,128)(2,1)S(1)} %add_convert_fusion.15), channel_id=1, source_target_pairs={{0,16},{4,20},{8,24},{12,28},{16,0},{20,4},{24,8},{28,12},{1,17},{... | collective-permute-start | bytes 786440 | tf_op jit(solution)/shard_map/ppermute | solution.py:51
  (93 other events, 1240.8 us)
